TPU v7x, 32 devices: a whole 2x2x4 slice. The times are simulated.
32 devices in a mesh: ctx: 16 (over z, x, core), tp: 2 (over y).
Axes of the slice: x: 2, y: 2, z: 4, core: 2. Of those that a mesh axis runs over, the one named last changes fastest.
Arguments:
- doc_lengths: int32 [32], replicated, may hold values from 1 to 512, 2048 in all
- ssm_x: bfloat16 [2048, 8192], P('ctx', 'tp'), may hold values from -6 to 6
- ssm_gate: bfloat16 [2048, 8192], P('ctx', 'tp'), may hold values from -6 to 6
- ssm_b: bfloat16 [2048, 2048], P('ctx', 'tp'), may hold values from -6 to 6
- ssm_c: bfloat16 [2048, 2048], P('ctx', 'tp'), may hold values from -0.375 to 0.375
- step_size: float32 [2048, 128], P('ctx', 'tp'), as said below
- decay_rate: float32 [128], P('tp'), as said below
- norm_weight: float32 [8192], P('tp'), may hold values from 0.1 to 1.9
- queries: bfloat16 [2048, 8192], P('ctx', 'tp'), may hold values from -96 to 96
- keys: bfloat16 [2048, 1024], P('ctx', 'tp'), may hold values from -4 to 4
- values: bfloat16 [2048, 1024], P('ctx', 'tp'), may hold values from -6 to 6
Outputs:
- mixed: bfloat16 [2048, 8192], P(('ctx', 'tp'))
- attended: bfloat16 [2048, 8192], P(('ctx', 'tp'))
Inputs may be any that keep to these rules, and one draw needn't show every extreme that they name: `doc_lengths`: every document has at least one token; the longest has exactly 512. `step_size`: Positive. `decay_rate`: Positive, at most 0.04.
All inputs are finite; a program needn't handle non-finite values.
Results may differ from a plain program's by a relative error of at most 0.0049.
Values may be sent and summed in bfloat16 or wider, within the bound.
A program may use at most 192 MiB of HBM per device.

v0:
```python
import jax
import jax.numpy as jnp
from jax import lax
from jax.sharding import PartitionSpec as P

HEADS = 128
GROUPS = 8
ATT_DIM = 128
DOC_DEVS = 4


NEG_LARGE = -1e30


def for_sending(x):
    return jax.tree.map(lambda a: a.astype(jnp.bfloat16) if a.dtype == jnp.float32 else a, x)


def passed_along(block, axis, distance):
    devices = range(lax.axis_size(axis))
    route = [(i - distance, i) for i in devices if i - distance in devices]
    return lax.ppermute(block, axis, route)


def doc_starts(doc_lengths):
    return jnp.cumsum(doc_lengths) - doc_lengths


def doc_index(positions, starts):
    return jnp.sum((starts[None, :] <= positions[:, None]).astype(jnp.int32), axis=1) - 1


def block_terms(ssm_x, ssm_b, ssm_c, step_size, decay_rate, doc_ids, prev_id, group_heads):
    tok_rows = ssm_x.shape[0]
    head_count = step_size.shape[1]
    group_count = head_count // group_heads
    head_size = ssm_x.shape[1] // head_count
    state_size = ssm_b.shape[1] // group_count
    inputs = ssm_x.reshape(tok_rows, group_count, group_heads, head_size)
    in_proj = ssm_b.reshape(tok_rows, group_count, state_size)
    out_proj = ssm_c.reshape(tok_rows, group_count, state_size)
    log_decay = -(step_size * decay_rate[None, :])
    cumulative = jnp.cumsum(log_decay, axis=0)
    same_doc = doc_ids[:, None] == doc_ids[None, :]
    causal = jnp.arange(tok_rows)[:, None] >= jnp.arange(tok_rows)[None, :]
    allowed = (same_doc & causal)[None]
    spread = cumulative.T[:, :, None] - cumulative.T[:, None, :]
    weights = (
        jnp.where(allowed, jnp.exp(jnp.where(allowed, spread, 0.0)), 0.0) * step_size.T[:, None, :]
    )
    intersection = jnp.einsum("tgn,sgn->gts", out_proj, in_proj, preferred_element_type=jnp.float32)
    mixing = (
        weights.reshape(group_count, group_heads, tok_rows, tok_rows) * intersection[:, None]
    ).astype(jnp.bfloat16)
    y_intra = jnp.einsum("ghts,sghp->tghp", mixing, inputs, preferred_element_type=jnp.float32)
    final_sum = cumulative[-1]
    tail = (
        jnp.exp(final_sum[None, :] - cumulative)
        * step_size
        * (doc_ids == doc_ids[-1]).astype(jnp.float32)[:, None]
    )
    scaled = (
        inputs.astype(jnp.float32) * tail.reshape(tok_rows, group_count, group_heads)[..., None]
    ).astype(jnp.bfloat16)
    state_local = jnp.einsum("sghp,sgn->ghpn", scaled, in_proj, preferred_element_type=jnp.float32)
    entry = jnp.exp(cumulative) * (doc_ids == prev_id).astype(jnp.float32)[:, None]
    transmit = jnp.exp(final_sum) * (doc_ids[-1] == prev_id).astype(jnp.float32)
    return (y_intra, state_local, entry, transmit.reshape(group_count, group_heads))


def finish_rows(y_intra, entry, carried, ssm_c, ssm_gate, norm_weight):
    tok_rows, group_count, group_heads, head_size = y_intra.shape
    out_proj = ssm_c.reshape(tok_rows, group_count, -1).astype(jnp.float32)
    incoming = jnp.einsum("tgn,ghpn->tghp", out_proj, carried, precision=lax.Precision.HIGHEST)
    mixer_out = y_intra + incoming * entry.reshape(tok_rows, group_count, group_heads)[..., None]
    gate_vals = ssm_gate.reshape(tok_rows, group_count, group_heads, head_size).astype(jnp.float32)
    gated = (mixer_out * jax.nn.silu(gate_vals)).reshape(
        tok_rows, group_count, group_heads * head_size
    )
    factor = lax.rsqrt(jnp.mean(gated * gated, axis=2, keepdims=True) + 1e-05)
    return ((gated * factor).reshape(tok_rows, -1) * norm_weight[None, :]).astype(jnp.bfloat16)


def chain_states(earlier, later):
    return (earlier[0] * later[0], later[0][:, :, None, None] * earlier[1] + later[1])


def attention_update(
    carry, query_rows, key_block, value_block, key_pos, query_pos, query_doc, starts
):
    running_max, running_sum, running_acc = carry
    block_rows = key_block.shape[0]
    kv_local = key_block.shape[1] // ATT_DIM
    key_heads = key_block.reshape(block_rows, kv_local, ATT_DIM)
    value_heads = value_block.reshape(block_rows, kv_local, ATT_DIM)
    key_doc = doc_index(key_pos, starts)
    allowed = (query_doc[:, None] == key_doc[None, :]) & (key_pos[None, :] <= query_pos[:, None])
    scores = jnp.einsum(
        "tngd,knd->ngtk", query_rows, key_heads, preferred_element_type=jnp.float32
    ) * ATT_DIM ** (-0.5)
    scores = jnp.where(allowed[None, None], scores, -jnp.inf)
    new_max = jnp.maximum(running_max, jnp.max(scores, axis=3))
    probs = jnp.exp(scores - new_max[..., None])
    factor = jnp.exp(running_max - new_max)
    new_sum = running_sum * factor + jnp.sum(probs, axis=3)
    weighted = jnp.einsum(
        "ngtk,knd->ngtd",
        probs.astype(jnp.bfloat16),
        value_heads,
        preferred_element_type=jnp.float32,
    )
    return (new_max, new_sum, running_acc * factor[..., None] + weighted)


def local(
    doc_lengths,
    ssm_x,
    ssm_gate,
    ssm_b,
    ssm_c,
    step_size,
    decay_rate,
    norm_weight,
    queries,
    keys,
    values,
):
    tok_rows = ssm_x.shape[0]
    ctx_index = lax.axis_index("ctx")
    begin = ctx_index * tok_rows
    positions = begin + jnp.arange(tok_rows, dtype=jnp.int32)
    starts = doc_starts(doc_lengths)
    doc_ids = doc_index(positions, starts)
    prev_id = doc_index(jnp.reshape(begin - 1, (1,)), starts)[0]
    group_heads = HEADS // GROUPS
    y_intra, state_local, entry, transmit = block_terms(
        ssm_x, ssm_b, ssm_c, step_size, decay_rate, doc_ids, prev_id, group_heads
    )
    merged = (transmit, state_local)
    for level_bit in range(DOC_DEVS.bit_length() - 1):
        earlier = passed_along(
            (for_sending(merged[0]), for_sending(merged[1])), "ctx", 1 << level_bit
        )
        merged = chain_states(earlier, merged)
    carried = passed_along(merged[1], "ctx", 1)
    mixed_rows = finish_rows(y_intra, entry, carried, ssm_c, ssm_gate, norm_weight)
    kv_local = keys.shape[1] // ATT_DIM
    q_groups = queries.shape[1] // (kv_local * ATT_DIM)
    query_rows = queries.reshape(tok_rows, kv_local, q_groups, ATT_DIM)
    floor_start = jnp.max(jnp.where(starts <= begin, starts, 0))
    query_last = begin + tok_rows - 1
    carry_shape = (kv_local, q_groups, tok_rows)
    initial = (
        jnp.full(carry_shape, NEG_LARGE, jnp.float32),
        jnp.zeros(carry_shape, jnp.float32),
        jnp.zeros(carry_shape + (ATT_DIM,), jnp.float32),
    )

    def visit(carry, key_block, value_block, key_begin):
        block_rows = key_block.shape[0]
        needed = (key_begin <= query_last) & (key_begin + block_rows - 1 >= floor_start)

        def update(inner):
            key_pos = key_begin + jnp.arange(block_rows, dtype=jnp.int32)
            return attention_update(
                inner, query_rows, key_block, value_block, key_pos, positions, doc_ids, starts
            )

        def unchanged(inner):
            return inner

        return lax.cond(needed, update, unchanged, carry)

    totals = visit(initial, keys, values, begin)
    for hop_count in range(1, DOC_DEVS + 1):
        near_keys, near_values = passed_along((keys, values), "ctx", hop_count)
        totals = visit(totals, near_keys, near_values, begin - hop_count * tok_rows)
    final_out = totals[2] / totals[1][..., None]
    attended_rows = (
        jnp.transpose(final_out, (2, 0, 1, 3)).reshape(tok_rows, -1).astype(jnp.bfloat16)
    )
    mixed_local, attended_local = (
        lax.all_to_all(mixed_rows, "tp", split_axis=0, concat_axis=1, tiled=True),
        lax.all_to_all(attended_rows, "tp", split_axis=0, concat_axis=1, tiled=True),
    )
    return (mixed_local, attended_local)


def solution(mesh):
    return jax.shard_map(
        local,
        mesh=mesh,
        in_specs=(
            P(),
            P("ctx", "tp"),
            P("ctx", "tp"),
            P("ctx", "tp"),
            P("ctx", "tp"),
            P("ctx", "tp"),
            P("tp"),
            P("tp"),
            P("ctx", "tp"),
            P("ctx", "tp"),
            P("ctx", "tp"),
        ),
        out_specs=(P(("ctx", "tp"), None), P(("ctx", "tp"), None)),
        check_vma=False,
    )
```

profile of v0, /device:TPU:19, one launch (start us, length us, event | category | flops | bytes accessed | tf_op | source)
XLA Modules:
  0.0 232.0 jit_solution(9776765901697887157)
XLA Ops:
  0.7 0.8 copy.164
  1.6 1.3 fusion.53
  5.7 0.8 copy.170
  6.6 0.8 multiply_negate_fusion
  8.4 1.6 copy.169
  10.2 3.4 %fusion.61 = (bf16[4,16,64,256]{3,2,1,0:T(8,128)(2,1)}, f32[4,16,64,256]{3,2,1,0:T(8,128)}) fusion(bf16[128,4,256,1]{2,1,0,3:T(4,128)(2,1)S(1)} %bitcast.87, bf16[128,4,16,64]{0,3,2,1:T(8,128)(2,1)S(1)} %bitcast.80, f32[128,4,16]{0,2,1:T(8,128)S(1)} %bitcast.100), kind=kOutput, calls=%fused_computation.124 | convolution fusion | flops 271056896 | bytes 7634944 | tf_op jit(solution)/shard_map/sghp,sgn->ghpn/dot_general | solution.py:65
  13.6 3.7 %collective-permute-start.1 = (bf16[4,16,64,256]{3,2,1,0:T(8,128)(2,1)}, bf16[4,16,64,256]{3,2,1,0:T(8,128)(2,1)S(1)}, u32[]{:S(2)}, u32[]{:S(2)}) collective-permute-start(bf16[4,16,64,256]{3,2,1,0:T(8,128)(2,1)} %get-tuple-element.410), channel_id=1, source_target_pairs={{0,2},{2,4},{4,6},{6,8},{8,10},{10,12},{12,14},{14,16},{16,18},{18... | collective-permute-start | bytes 6291464 | tf_op jit(solution)/shard_map/ppermute | solution.py:22
  18.0 22.5 %collective-permute-done.1 = bf16[4,16,64,256]{3,2,1,0:T(8,128)(2,1)S(1)} collective-permute-done((bf16[4,16,64,256]{3,2,1,0:T(8,128)(2,1)}, bf16[4,16,64,256]{3,2,1,0:T(8,128)(2,1)S(1)}, u32[]{:S(2)}, u32[]{:S(2)}) %collective-permute-start.1) | collective-permute-done | bytes 2097184 | tf_op jit(solution)/shard_map/ppermute | solution.py:22
  40.6 2.9 %fusion.31 = bf16[4,16,64,256]{3,2,1,0:T(8,128)(2,1)S(1)} fusion(f32[4,16,64,256]{3,2,1,0:T(8,128)} %get-tuple-element.411, bf16[4,16,64,256]{3,2,1,0:T(8,128)(2,1)S(1)} %collective-permute-done.1, f32[4,16]{1,0:T(4,128)S(1)} %mul.225), kind=kLoop, calls=%fused_computation.74 | loop fusion | flops 4194304 | bytes 8388864 | tf_op jit(solution)/shard_map/convert_element_type | solution.py:16
  43.5 3.1 %collective-permute-start.2 = (bf16[4,16,64,256]{3,2,1,0:T(8,128)(2,1)S(1)}, bf16[4,16,64,256]{3,2,1,0:T(8,128)(2,1)S(1)}, u32[]{:S(2)}, u32[]{:S(2)}) collective-permute-start(bf16[4,16,64,256]{3,2,1,0:T(8,128)(2,1)S(1)} %fusion.31), channel_id=1, source_target_pairs={{0,4},{2,6},{4,8},{6,10},{8,12},{10,14},{12,16},{14,18},{16,20},{1... | collective-permute-start | bytes 6291464 | tf_op jit(solution)/shard_map/ppermute | solution.py:22
  46.6 4.6 %collective-permute-start = (bf16[4,16]{1,0:T(4,128)(2,1)S(1)}, bf16[4,16]{1,0:T(4,128)(2,1)S(1)}, u32[]{:S(2)}, u32[]{:S(2)}) collective-permute-start(bf16[4,16]{1,0:T(4,128)(2,1)S(1)} %convert_element_type.121), channel_id=1, source_target_pairs={{0,2},{2,4},{4,6},{6,8},{8,10},{10,12},{12,14},{14,16},{16,18},{18... | collective-permute-start | bytes 392 | tf_op jit(solution)/shard_map/ppermute | solution.py:22
  51.2 38.2 %collective-permute-done = bf16[4,16]{1,0:T(4,128)(2,1)S(1)} collective-permute-done((bf16[4,16]{1,0:T(4,128)(2,1)S(1)}, bf16[4,16]{1,0:T(4,128)(2,1)S(1)}, u32[]{:S(2)}, u32[]{:S(2)}) %collective-permute-start) | collective-permute-done | bytes 160 | tf_op jit(solution)/shard_map/ppermute | solution.py:22
  89.4 1.9 collective-permute-done.2
  91.3 2.8 %multiply_add_fusion.8 = f32[4,16,64,256]{3,2,1,0:T(8,128)} fusion(bf16[4,16,64,256]{3,2,1,0:T(8,128)(2,1)S(1)} %collective-permute-done.2, f32[4,16,64,256]{3,2,1,0:T(8,128)S(1)} %copy-done, bf16[4,16,64,256]{3,2,1,0:T(8,128)(2,1)S(1)} %collective-permute-done.1, f32[4,16]{1,0:T(4,128)S(1)} %mul.225, f32[4,16]{1,0:T(4,128)S(1)} %convert_multiply_fusion), kind=kLoop, calls=%fused_computation.71 | loop fusion | flops 6291456 | bytes 12583424 | tf_op jit(solution)/shard_map/add | solution.py:85
  94.2 6.0 %collective-permute-start.3 = (f32[4,16,64,256]{3,2,1,0:T(8,128)}, f32[4,16,64,256]{3,2,1,0:T(8,128)}, u32[]{:S(2)}, u32[]{:S(2)}) collective-permute-start(f32[4,16,64,256]{3,2,1,0:T(8,128)} %multiply_add_fusion.8), channel_id=1, source_target_pairs={{0,2},{2,4},{4,6},{6,8},{8,10},{10,12},{12,14},{14,16},{16,18},{18... | collective-permute-start | bytes 12582920 | tf_op jit(solution)/shard_map/ppermute | solution.py:22
  100.2 1.9 collective-permute-start.4
  102.1 1.9 collective-permute-start.6
  104.0 1.9 collective-permute-start.5
  106.0 1.9 collective-permute-start.7
  108.1 1.2 fusion.44
  109.3 4.2 %fusion.32 = f32[4,16,128,64]{2,3,1,0:T(8,128)} fusion(bf16[128,4,16,64]{0,3,2,1:T(8,128)(2,1)S(1)} %bitcast.81, f32[4,128,128]{2,1,0:T(8,128)S(1)} %fusion.44, f32[4,16,128]{2,1,0:T(8,128)} %bitcast.101, f32[4,16,128]{2,1,0:T(8,128)S(1)} %bitcast.103, pred[128,128]{1,0:T(8,128)(4,1)S(1)} %fusion.51), kind=kOutput, calls=%fused_computation.75 | convolution fusion | flops 140509184 | bytes 3489792 | tf_op jit(solution)/shard_map/ghts,sghp->tghp/dot_general | solution.py:55
  114.8 0.9 reshape.555
  115.7 1.6 copy.179
  119.4 1.6 copy.175
  121.0 7.4 %conditional.5 = (f32[4,8,128]{2,1,0:T(8,128)}, f32[4,8,128]{2,1,0:T(8,128)S(1)}, f32[4,8,128,128]{3,2,1,0:T(8,128)S(1)}) conditional(s32[]{:T(128)} %convert_element_type.138, () %tuple.41, (s32[128]{0:T(128)S(1)}, s32[32]{0:T(128)S(1)}, s32[]{:T(128)}, s32[128]{0:T(128)S(1)}, bf16[128,512]{1,0:T(8,128)(2,1)}, ...), branch_computations={%region_6.7_spmd, %region_7.11_spmd} | conditional | flops 272707712 | bytes 18830008 | solution.py:172
  121.2 0.9 reshape.536
  123.3 1.1 fusion.1
  125.1 0.9 reshape.537
  126.1 2.3 convolution_add_fusion
  128.4 21.7 %collective-permute-done.4 = bf16[128,512]{1,0:T(8,128)(2,1)} collective-permute-done((bf16[128,512]{1,0:T(8,128)(2,1)}, bf16[128,512]{1,0:T(8,128)(2,1)}, u32[]{:S(2)}, u32[]{:S(2)}) %collective-permute-start.4) | collective-permute-done | bytes 131104 | tf_op jit(solution)/shard_map/ppermute | solution.py:22
  150.1 2.3 collective-permute-start.8
  152.9 2.3 collective-permute-start.9
  155.3 1.9 collective-permute-start.10
  157.2 1.9 collective-permute-start.11
  159.1 8.1 %conditional.6 = ((f32[4,8,128]{2,1,0:T(8,128)}, f32[4,8,128]{2,1,0:T(8,128)S(1)}, f32[4,8,128,128]{3,2,1,0:T(8,128)S(1)})) conditional(s32[]{:T(128)} %convert_element_type.137, (f32[4,8,128]{2,1,0:T(8,128)}, f32[4,8,128]{2,1,0:T(8,128)S(1)}, f32[4,8,128,128]{3,2,1,0:T(8,128)S(1)}) %conditional.5, (s32[128]{0:T(128)S(1)}, s32[32]{0:T(128)S(1)}, ...), branch_computations={%region_11.12_spmd, %region_12.16_spmd} | conditional | flops 273223808 | bytes 21009088 | solution.py:172
  159.4 0.9 reshape.538
  160.8 0.7 max.8
  163.3 0.9 reshape.539
  164.2 2.4 %multiply_add_fusion = f32[4,8,128,128]{3,2,1,0:T(8,128)S(1)} fusion(f32[4,8,128,128]{3,2,1,0:T(8,128)S(1)} %get-tuple-element.131, f32[4,8,128,128]{2,3,1,0:T(8,128)} %copy-done.1, f32[4,8,128]{2,1,0:T(8,128)S(1)} %get-tuple-element.386, f32[4,8,128]{2,1,0:T(8,128)S(1)} %max.8, bf16[128,4,128,1]{2,1,0,3:T(4,128)(2,1)S(1)} %bitcast.92), kind=kOutput, calls=%fused_computation.16 | convolution fusion | flops 136314880 | bytes 6455296 | tf_op jit(solution)/shard_map/cond/branch_1_fun/ngtk,knd->ngtd/dot_general | solution.py:106
  167.2 8.0 %conditional.7 = ((f32[4,8,128]{2,1,0:T(8,128)}, f32[4,8,128]{2,1,0:T(8,128)S(1)}, f32[4,8,128,128]{3,2,1,0:T(8,128)S(1)})) conditional(s32[]{:T(128)} %convert_element_type.136, (f32[4,8,128]{2,1,0:T(8,128)}, f32[4,8,128]{2,1,0:T(8,128)S(1)}, f32[4,8,128,128]{3,2,1,0:T(8,128)S(1)}) %get-tuple-element.442, (s32[128]{0:T(128)S(1)}, ...), branch_computations={%region_16.17_spmd, %region_17.21_spmd} | conditional | flops 273223808 | bytes 21009088 | solution.py:172
  167.4 0.9 reshape.540
  171.3 0.9 reshape.541
  172.2 2.4 %multiply_add_fusion.2 = f32[4,8,128,128]{3,2,1,0:T(8,128)S(1)} fusion(f32[4,8,128,128]{3,2,1,0:T(8,128)S(1)} %get-tuple-element.141, f32[4,8,128,128]{2,3,1,0:T(8,128)} %copy-done.2, f32[4,8,128]{2,1,0:T(8,128)S(1)} %get-tuple-element.388, f32[4,8,128]{2,1,0:T(8,128)S(1)} %max.9, bf16[128,4,128,1]{2,1,0,3:T(4,128)(2,1)S(1)} %bitcast.94), kind=kOutput, calls=%fused_computation.30 | convolution fusion | flops 136314880 | bytes 6455296 | tf_op jit(solution)/shard_map/cond/branch_1_fun/ngtk,knd->ngtd/dot_general | solution.py:106
  175.2 8.0 %conditional.8 = ((f32[4,8,128]{2,1,0:T(8,128)}, f32[4,8,128]{2,1,0:T(8,128)S(1)}, f32[4,8,128,128]{3,2,1,0:T(8,128)S(1)})) conditional(s32[]{:T(128)} %convert_element_type.135, (f32[4,8,128]{2,1,0:T(8,128)}, f32[4,8,128]{2,1,0:T(8,128)S(1)}, f32[4,8,128,128]{3,2,1,0:T(8,128)S(1)}) %get-tuple-element.443, (s32[128]{0:T(128)S(1)}, ...), branch_computations={%region_21.22_spmd, %region_22.26_spmd} | conditional | flops 273223808 | bytes 21009088 | solution.py:172
  175.4 0.9 reshape.542
  176.8 0.7 max.10
  179.3 0.9 reshape.543
  180.3 2.4 %multiply_add_fusion.4 = f32[4,8,128,128]{3,2,1,0:T(8,128)S(1)} fusion(f32[4,8,128,128]{3,2,1,0:T(8,128)S(1)} %get-tuple-element.151, f32[4,8,128,128]{2,3,1,0:T(8,128)} %copy-done.3, f32[4,8,128]{2,1,0:T(8,128)S(1)} %get-tuple-element.390, f32[4,8,128]{2,1,0:T(8,128)S(1)} %max.10, bf16[128,4,128,1]{2,1,0,3:T(4,128)(2,1)S(1)} %bitcast.96), kind=kOutput, calls=%fused_computation.44 | convolution fusion | flops 136314880 | bytes 6455296 | tf_op jit(solution)/shard_map/cond/branch_1_fun/ngtk,knd->ngtd/dot_general | solution.py:106
  183.3 6.5 %conditional.9 = ((f32[4,8,128]{2,1,0:T(8,128)S(1)}, f32[4,8,128,128]{3,2,1,0:T(8,128)S(1)})) conditional(s32[]{:T(128)} %convert_element_type.134, (f32[4,8,128]{2,1,0:T(8,128)S(1)}, f32[4,8,128,128]{3,2,1,0:T(8,128)S(1)}) %tuple.46, (s32[128]{0:T(128)S(1)}, s32[32]{0:T(128)S(1)}, s32[]{:T(128)}, s32[128]{0:T(128)S(1)}, ...), branch_computations={%region_26.27_spmd, %region_27.31_spmd} | conditional | flops 273223808 | bytes 20976312 | solution.py:172
  184.0 0.7 max.11
  186.5 0.9 reshape.545
  187.4 2.4 %multiply_add_fusion.6 = f32[4,8,128,128]{3,2,1,0:T(8,128)S(1)} fusion(f32[4,8,128,128]{3,2,1,0:T(8,128)S(1)} %get-tuple-element.161, f32[4,8,128,128]{2,3,1,0:T(8,128)} %copy-done.4, f32[4,8,128]{2,1,0:T(8,128)S(1)} %get-tuple-element.392, f32[4,8,128]{2,1,0:T(8,128)S(1)} %max.11, bf16[128,4,128,1]{2,1,0,3:T(4,128)(2,1)S(1)} %bitcast.89), kind=kOutput, calls=%fused_computation.58 | convolution fusion | flops 136314880 | bytes 6455296 | tf_op jit(solution)/shard_map/cond/branch_1_fun/ngtk,knd->ngtd/dot_general | solution.py:106
  191.2 1.3 convert_element_type.141
  192.5 3.6 %all-to-all-start.1 = ((bf16[2,64,4096]{2,1,0:T(8,128)(2,1)}), bf16[2,64,4096]{2,1,0:T(8,128)(2,1)S(1)}, u32[]{:S(2)}, u32[]{:S(2)}) async-start(bf16[2,64,4096]{2,1,0:T(8,128)(2,1)} %convert_element_type.141), calls=%async_computation.1 | async-start | bytes 2097152 | tf_op jit(solution)/shard_map/all_to_all | solution.py:184
  196.1 5.8 %multiply_reduce_fusion = (f32[128,4]{0,1:T(4,128)S(1)}, f32[128,4,16,64]{0,3,2,1:T(8,128)S(1)}) fusion(f32[128,4,16,64]{0,3,2,1:T(8,128)} %bitcast.82, f32[128,4,16]{0,2,1:T(8,128)S(1)} %broadcast_multiply_fusion, f32[4,16,64,256]{3,2,1,0:T(8,128)} %collective-permute-done.3, bf16[128,4,256,1]{2,1,0,3:T(4,128)(2,1)S(1)} %bitcast.99, ...), kind=kOutput, calls=%fused_computation.81 | convolution fusion | flops 1615330816 | bytes 10782720 | tf_op jit(solution)/shard_map/tgn,ghpn->tghp/dot_general | solution.py:74
  201.9 3.7 %reshape.573 = f32[2,64,4096]{1,0,2:T(2,128)} reshape(f32[128,4,16,64]{0,3,2,1:T(8,128)S(1)} %get-tuple-element.413) | data formatting | bytes 4194304 | tf_op jit(solution)/shard_map/reshape | solution.py:77
  205.5 5.3 %copy.233 = f32[2,64,4096]{2,1,0:T(8,128)S(1)} copy(f32[2,64,4096]{1,0,2:T(2,128)} %reshape.573) | data formatting | bytes 4194304 | tf_op jit(solution)/shard_map/reshape | solution.py:77
  211.0 1.7 mul.244
  212.7 3.7 %mul.245 = f32[2,64,4096]{2,1,0:T(8,128)} reshape(f32[128,4,1024]{2,1,0:T(4,128)} %mul.244) | data formatting | bytes 4194304 | tf_op jit(solution)/shard_map/mul | solution.py:81
  216.3 2.8 %multiply_convert_fusion.2 = bf16[2,64,4096]{2,1,0:T(8,128)(2,1)} fusion(f32[2,64,4096]{2,1,0:T(8,128)S(1)} %copy.233, f32[2,64,4096]{2,1,0:T(8,128)} %mul.245, f32[4096]{0:T(1024)S(1)} %copy-done.10), kind=kLoop, calls=%fused_computation.80 | loop fusion | flops 1572864 | bytes 5259264 | tf_op jit(solution)/shard_map/convert_element_type | solution.py:81
  219.2 3.6 %all-to-all-start = ((bf16[2,64,4096]{2,1,0:T(8,128)(2,1)}), bf16[2,64,4096]{2,1,0:T(8,128)(2,1)S(1)}, u32[]{:S(2)}, u32[]{:S(2)}) async-start(bf16[2,64,4096]{2,1,0:T(8,128)(2,1)} %multiply_convert_fusion.2), calls=%async_computation | async-start | bytes 2097152 | tf_op jit(solution)/shard_map/all_to_all | solution.py:183
  222.7 1.1 copy.237
  223.8 7.2 %all-to-all-done = bf16[2,64,4096]{2,1,0:T(8,128)(2,1)S(1)} async-done(((bf16[2,64,4096]{2,1,0:T(8,128)(2,1)}), bf16[2,64,4096]{2,1,0:T(8,128)(2,1)S(1)}, u32[]{:S(2)}, u32[]{:S(2)}) %all-to-all-start) | async-done | bytes 1048608 | tf_op jit(solution)/shard_map/all_to_all | solution.py:183
  231.0 1.1 copy.236
  (99 shorter events, 19.9 us)
Async XLA Ops:
  0.6 9.4 %copy-start.7 = (bf16[128,1024]{1,0:T(8,128)(2,1)S(1)}, bf16[128,1024]{1,0:T(8,128)(2,1)}, u32[]{:S(2)}) copy-start(bf16[128,1024]{1,0:T(8,128)(2,1)} %param.24) | copy-start | bytes 786436
  2.9 4.5 %copy-start.11 = (s32[32]{0:T(128)}, s32[32]{0:T(128)S(1)}, u32[]{:S(2)}) copy-start(s32[32]{0:T(128)S(1)} %get-tuple-element.393) | copy-start | bytes 388
  13.6 27.0 %collective-permute-start.1 = (bf16[4,16,64,256]{3,2,1,0:T(8,128)(2,1)}, bf16[4,16,64,256]{3,2,1,0:T(8,128)(2,1)S(1)}, u32[]{:S(2)}, u32[]{:S(2)}) collective-permute-start(bf16[4,16,64,256]{3,2,1,0:T(8,128)(2,1)} %get-tuple-element.410), channel_id=1, source_target_pairs={{0,2},{2,4},{4,6},{6,8},{8,10},{10,12},{12,14},{14,16},{16,18},{18... | collective-permute-start | bytes 6291464 | tf_op jit(solution)/shard_map/ppermute | solution.py:22
  40.6 50.8 %copy-start = (f32[4,16,64,256]{3,2,1,0:T(8,128)S(1)}, f32[4,16,64,256]{3,2,1,0:T(8,128)}, u32[]{:S(2)}) copy-start(f32[4,16,64,256]{3,2,1,0:T(8,128)} %get-tuple-element.411) | copy-start | bytes 12582916
  43.5 47.9 %collective-permute-start.2 = (bf16[4,16,64,256]{3,2,1,0:T(8,128)(2,1)S(1)}, bf16[4,16,64,256]{3,2,1,0:T(8,128)(2,1)S(1)}, u32[]{:S(2)}, u32[]{:S(2)}) collective-permute-start(bf16[4,16,64,256]{3,2,1,0:T(8,128)(2,1)S(1)} %fusion.31), channel_id=1, source_target_pairs={{0,4},{2,6},{4,8},{6,10},{8,12},{10,14},{12,16},{14,18},{16,20},{1... | collective-permute-start | bytes 6291464 | tf_op jit(solution)/shard_map/ppermute | solution.py:22
  46.6 42.8 %collective-permute-start = (bf16[4,16]{1,0:T(4,128)(2,1)S(1)}, bf16[4,16]{1,0:T(4,128)(2,1)S(1)}, u32[]{:S(2)}, u32[]{:S(2)}) collective-permute-start(bf16[4,16]{1,0:T(4,128)(2,1)S(1)} %convert_element_type.121), channel_id=1, source_target_pairs={{0,2},{2,4},{4,6},{6,8},{8,10},{10,12},{12,14},{14,16},{16,18},{18... | collective-permute-start | bytes 392 | tf_op jit(solution)/shard_map/ppermute | solution.py:22
  94.2 101.9 %collective-permute-start.3 = (f32[4,16,64,256]{3,2,1,0:T(8,128)}, f32[4,16,64,256]{3,2,1,0:T(8,128)}, u32[]{:S(2)}, u32[]{:S(2)}) collective-permute-start(f32[4,16,64,256]{3,2,1,0:T(8,128)} %multiply_add_fusion.8), channel_id=1, source_target_pairs={{0,2},{2,4},{4,6},{6,8},{8,10},{10,12},{12,14},{14,16},{16,18},{18... | collective-permute-start | bytes 12582920 | tf_op jit(solution)/shard_map/ppermute | solution.py:22
  100.2 50.0 %collective-permute-start.4 = (bf16[128,512]{1,0:T(8,128)(2,1)}, bf16[128,512]{1,0:T(8,128)(2,1)}, u32[]{:S(2)}, u32[]{:S(2)}) collective-permute-start(bf16[128,512]{1,0:T(8,128)(2,1)} %param.30), channel_id=1, source_target_pairs={{0,2},{2,4},{4,6},{6,8},{8,10},{10,12},{12,14},{14,16},{16,18},{18... | collective-permute-start | bytes 393224 | tf_op jit(solution)/shard_map/ppermute | solution.py:22
  102.1 53.2 %collective-permute-start.6 = (bf16[128,512]{1,0:T(8,128)(2,1)}, bf16[128,512]{1,0:T(8,128)(2,1)}, u32[]{:S(2)}, u32[]{:S(2)}) collective-permute-start(bf16[128,512]{1,0:T(8,128)(2,1)} %param.30), channel_id=1, source_target_pairs={{0,4},{2,6},{4,8},{6,10},{8,12},{10,14},{12,16},{14,18},{16,20},{1... | collective-permute-start | bytes 393224 | tf_op jit(solution)/shard_map/ppermute | solution.py:22
  104.0 48.9 %collective-permute-start.5 = (bf16[128,512]{1,0:T(8,128)(2,1)}, bf16[128,512]{1,0:T(8,128)(2,1)}, u32[]{:S(2)}, u32[]{:S(2)}) collective-permute-start(bf16[128,512]{1,0:T(8,128)(2,1)} %param.31), channel_id=1, source_target_pairs={{0,2},{2,4},{4,6},{6,8},{8,10},{10,12},{12,14},{14,16},{16,18},{18... | collective-permute-start | bytes 393224 | tf_op jit(solution)/shard_map/ppermute | solution.py:22
  106.0 51.2 %collective-permute-start.7 = (bf16[128,512]{1,0:T(8,128)(2,1)}, bf16[128,512]{1,0:T(8,128)(2,1)}, u32[]{:S(2)}, u32[]{:S(2)}) collective-permute-start(bf16[128,512]{1,0:T(8,128)(2,1)} %param.31), channel_id=1, source_target_pairs={{0,4},{2,6},{4,8},{6,10},{8,12},{10,14},{12,16},{14,18},{16,20},{1... | collective-permute-start | bytes 393224 | tf_op jit(solution)/shard_map/ppermute | solution.py:22
  109.2 5.6 %copy-start.8 = (bf16[128,1024]{1,0:T(8,128)(2,1)S(1)}, bf16[128,1024]{1,0:T(8,128)(2,1)}, u32[]{:S(2)}) copy-start(bf16[128,1024]{1,0:T(8,128)(2,1)} %param.25) | copy-start | bytes 786436
  113.4 6.0 %copy-start.6 = (bf16[128,4096]{1,0:T(8,128)(2,1)S(1)}, bf16[128,4096]{1,0:T(8,128)(2,1)}, u32[]{:S(2)}) copy-start(bf16[128,4096]{1,0:T(8,128)(2,1)} %param.23) | copy-start | bytes 3145732
  113.4 6.0 %copy-start.12 = (s32[32]{0:T(128)S(1)}, s32[32]{0:T(128)}, u32[]{:S(2)}) copy-start(s32[32]{0:T(128)} %copy-done.11) | copy-start | bytes 388
  122.6 3.5 %copy-start.5 = (f32[4,8,128,128]{2,3,1,0:T(8,128)}, f32[4,8,128,128]{2,3,1,0:T(8,128)S(1)}, u32[]{:S(2)}) copy-start(f32[4,8,128,128]{2,3,1,0:T(8,128)S(1)} %get-tuple-element.395) | copy-start | bytes 6291460 | tf_op jit(solution)/shard_map/cond
  150.1 25.1 %collective-permute-start.8 = (bf16[128,512]{1,0:T(8,128)(2,1)}, bf16[128,512]{1,0:T(8,128)(2,1)}, u32[]{:S(2)}, u32[]{:S(2)}) collective-permute-start(bf16[128,512]{1,0:T(8,128)(2,1)} %param.30), channel_id=1, source_target_pairs={{0,6},{2,8},{4,10},{6,12},{8,14},{10,16},{12,18},{14,20},{16,22},{... | collective-permute-start | bytes 393224 | tf_op jit(solution)/shard_map/ppermute | solution.py:22
  152.9 22.3 %collective-permute-start.9 = (bf16[128,512]{1,0:T(8,128)(2,1)}, bf16[128,512]{1,0:T(8,128)(2,1)}, u32[]{:S(2)}, u32[]{:S(2)}) collective-permute-start(bf16[128,512]{1,0:T(8,128)(2,1)} %param.31), channel_id=1, source_target_pairs={{0,6},{2,8},{4,10},{6,12},{8,14},{10,16},{12,18},{14,20},{16,22},{... | collective-permute-start | bytes 393224 | tf_op jit(solution)/shard_map/ppermute | solution.py:22
  155.3 28.0 %collective-permute-start.10 = (bf16[128,512]{1,0:T(8,128)(2,1)}, bf16[128,512]{1,0:T(8,128)(2,1)S(1)}, u32[]{:S(2)}, u32[]{:S(2)}) collective-permute-start(bf16[128,512]{1,0:T(8,128)(2,1)} %param.30), channel_id=1, source_target_pairs={{0,8},{2,10},{4,12},{6,14},{8,16},{10,18},{12,20},{14,22},{16,24},... | collective-permute-start | bytes 393224 | tf_op jit(solution)/shard_map/ppermute | solution.py:22
  157.2 26.1 %collective-permute-start.11 = (bf16[128,512]{1,0:T(8,128)(2,1)}, bf16[128,512]{1,0:T(8,128)(2,1)}, u32[]{:S(2)}, u32[]{:S(2)}) collective-permute-start(bf16[128,512]{1,0:T(8,128)(2,1)} %param.31), channel_id=1, source_target_pairs={{0,8},{2,10},{4,12},{6,14},{8,16},{10,18},{12,20},{14,22},{16,24},... | collective-permute-start | bytes 393224 | tf_op jit(solution)/shard_map/ppermute | solution.py:22
  160.8 1.4 copy-start.1
  168.8 1.4 copy-start.2
  176.8 1.4 copy-start.3
  184.0 1.4 copy-start.4
  191.2 4.9 %copy-start.9 = (bf16[128,4,256]{2,1,0:T(4,128)(2,1)S(1)}, bf16[128,4,256]{2,1,0:T(4,128)(2,1)}, u32[]{:S(2)}) copy-start(bf16[128,4,256]{2,1,0:T(4,128)(2,1)} %reshape.555) | copy-start | bytes 786436
  192.5 26.7 %all-to-all-start.1 = ((bf16[2,64,4096]{2,1,0:T(8,128)(2,1)}), bf16[2,64,4096]{2,1,0:T(8,128)(2,1)S(1)}, u32[]{:S(2)}, u32[]{:S(2)}) async-start(bf16[2,64,4096]{2,1,0:T(8,128)(2,1)} %convert_element_type.141), calls=%async_computation.1 | async-start | bytes 2097152 | tf_op jit(solution)/shard_map/all_to_all | solution.py:184
  212.7 3.7 %copy-start.10 = (f32[4096]{0:T(1024)S(1)}, f32[4096]{0:T(1024)}, u32[]{:S(2)}) copy-start(f32[4096]{0:T(1024)} %param.28) | copy-start | bytes 49156
  219.2 11.8 %all-to-all-start = ((bf16[2,64,4096]{2,1,0:T(8,128)(2,1)}), bf16[2,64,4096]{2,1,0:T(8,128)(2,1)S(1)}, u32[]{:S(2)}, u32[]{:S(2)}) async-start(bf16[2,64,4096]{2,1,0:T(8,128)(2,1)} %multiply_convert_fusion.2), calls=%async_computation | async-start | bytes 2097152 | tf_op jit(solution)/shard_map/all_to_all | solution.py:183
where the time goes:
time: 232 us
  waiting for transfers between devices  92.1 us (40%)
  starting transfers between devices  40.7 us (18%)
  local copies, waits for them, and re-layouts  40.5 us (17%)
  matrix products  28.5 us (12%)
  other arithmetic  24.3 us (10%)
  between operations  5.7 us (2%)
    ppermute x12, waiting for transfers between devices, passed_along(): return lax.ppermute(block, axis, route)  84.9 us
    ppermute x12, starting transfers between devices, passed_along(): return lax.ppermute(block, axis, route)  33.5 us
    dot_general x5, matrix products, attention_update(): jnp.einsum('ngtk,knd->ngtd', probs.astype(jnp.bfloat16), value_heads, pre...  11.8 us
    reshape x2, local copies, waits for them, and re-layouts, finish_rows(): (mixer_out * jax.nn.silu(gate_vals)).reshape(tok_rows, group_count, group...  8.96 us
    all_to_all x1, waiting for transfers between devices, local(): lax.all_to_all(mixed_rows, 'tp', split_axis=0, concat_axis=1, tiled=True)  7.16 us
    dot_general x1, matrix products, finish_rows(): jnp.einsum('tgn,ghpn->tghp', out_proj, carried, precision=lax.Precision.H...  5.78 us
    mul x2, local copies, waits for them, and re-layouts, finish_rows(): gated * factor  5.36 us
    reshape x5, local copies, waits for them, and re-layouts, attention_update(): value_heads = value_block.reshape(block_rows, kv_local, ATT_DIM)  4.7 us
  transfers between devices with their start and end apart: 14, of which 6 were waited for; matrix products, arithmetic and copies ran while one was open for 31% of the time, Pallas kernels for 0%

commit v1 on v0

--- a/solution.py
+++ b/solution.py
@@ -1,6 +1,8 @@
 import jax
 import jax.numpy as jnp
 from jax import lax
+from jax.experimental import pallas as pl
+from jax.experimental.pallas import tpu as pltpu
 from jax.sharding import PartitionSpec as P
 
 HEADS = 128
@@ -112,7 +114,7 @@
     return (new_max, new_sum, running_acc * factor[..., None] + weighted)
 
 
-def local(
+def local_any(
     doc_lengths,
     ssm_x,
     ssm_gate,
@@ -186,9 +188,318 @@
     return (mixed_local, attended_local)
 
 
+LOG2E = 1.4426950408889634
+F32 = jnp.float32
+BF16 = jnp.bfloat16
+
+
+def dot(a, b, dims=(((1,), (0,)), ((), ()))):
+    return lax.dot_general(a, b, dims, preferred_element_type=F32)
+
+
+def stacked(first, own, received):
+    return jnp.where(first, own, received), jnp.where(first, received, own)
+
+
+def spread_heads(columns, tile, lanes, head_size):
+    per = lanes // head_size
+    lane = lax.broadcasted_iota(jnp.int32, (columns.shape[0], lanes), 1)
+    wide = jnp.broadcast_to(columns[:, tile * per : tile * per + 1], lane.shape)
+    for k in range(1, per):
+        column = columns[:, tile * per + k : tile * per + k + 1]
+        wide = jnp.where(lane >= k * head_size, column, wide)
+    return wide
+
+
+def state_kernel(x_ref, b_ref, tail_ref, s_ref, scaled):
+    heads = tail_ref.shape[2]
+    width = x_ref.shape[1]
+    tail = tail_ref[0]
+    for tile in range(width // 128):
+        cols = slice(tile * 128, tile * 128 + 128)
+        wide = spread_heads(tail, tile, 128, width // heads)
+        scaled[:, cols] = (x_ref[:, cols].astype(F32) * wide).astype(BF16)
+    s_ref[...] = dot(b_ref[...], scaled[...], (((0,), (0,)), ((), ()))).astype(BF16)
+
+
+def intra_kernel(x_ref, b_ref, c_ref, l_ref, lt_ref, dtt_ref, dq_ref, dk_ref, y_ref):
+    rows, width = x_ref.shape
+    heads = l_ref.shape[2]
+    head_size = width // heads
+    at = lax.broadcasted_iota(jnp.int32, (rows, rows), 0)
+    to = lax.broadcasted_iota(jnp.int32, (rows, rows), 1)
+    bias = jnp.where((dq_ref[...] == dk_ref[...]) & (to <= at), 0.0, NEG_LARGE)
+    inter = dot(c_ref[...], b_ref[...], (((1,), (1,)), ((), ())))
+    lcol, lrow, step = l_ref[0], lt_ref[0], dtt_ref[0]
+    per = 128 // head_size
+    lane = lax.broadcasted_iota(jnp.int32, (rows, 128), 1)
+    for tile in range(width // 128):
+        cols = slice(tile * 128, tile * 128 + 128)
+        total = None
+        for k in range(per):
+            h = tile * per + k
+            w = jnp.exp((lcol[:, h : h + 1] - lrow[h : h + 1, :]) + bias)
+            mix = (w * step[h : h + 1, :] * inter).astype(BF16)
+            part = dot(mix, x_ref[:, cols])
+            total = part if k == 0 else jnp.where(lane >= k * head_size, part, total)
+        y_ref[:, cols] = total
+
+
+def finish_kernel(y_ref, c_ref, s1_ref, s2_ref, t_ref, entry_ref, gate_ref, w_ref, o_ref, gated):
+    rows, width = y_ref.shape
+    heads = entry_ref.shape[2]
+    entry = entry_ref[0]
+    carried = (
+        s1_ref[...].astype(F32) + t_ref[...] * s2_ref[...].astype(F32)
+    ).astype(BF16)
+    gated[...] = dot(c_ref[...], carried)
+    square = jnp.zeros((rows, 128), F32)
+    for tile in range(width // 128):
+        cols = slice(tile * 128, tile * 128 + 128)
+        wide = spread_heads(entry, tile, 128, width // heads)
+        z = gate_ref[:, cols].astype(F32)
+        out = (y_ref[:, cols] + gated[:, cols] * wide) * (z / (1.0 + jnp.exp(-z)))
+        gated[:, cols] = out
+        square += out * out
+    mean = jnp.sum(square, axis=1, keepdims=True) * (1.0 / width)
+    factor = lax.rsqrt(mean + 1e-05)
+    o_ref[...] = (gated[...] * factor * w_ref[...]).astype(BF16)
+
+
+def attention_kernel(q_ref, k2_ref, v2_ref, k1_ref, v1_ref, k0_ref, v0_ref, dq_ref, dk_ref, o_ref):
+    rows, width = q_ref.shape
+    total_keys = 3 * rows
+    keys = jnp.concatenate([k2_ref[...], k1_ref[...], k0_ref[...]], axis=0)
+    vals = jnp.concatenate([v2_ref[...], v1_ref[...], v0_ref[...]], axis=0)
+    at = lax.broadcasted_iota(jnp.int32, (rows, total_keys), 0) + 2 * rows
+    to = lax.broadcasted_iota(jnp.int32, (rows, total_keys), 1)
+    bias = jnp.where((dq_ref[...] == dk_ref[...]) & (to <= at), 0.0, NEG_LARGE)
+    scale = LOG2E * ATT_DIM ** (-0.5)
+    for head in range(width // ATT_DIM):
+        cols = slice(head * ATT_DIM, (head + 1) * ATT_DIM)
+        scores = dot(q_ref[:, cols], keys, (((1,), (1,)), ((), ()))) + bias
+        top = jnp.max(scores, axis=1, keepdims=True)
+        probs = jnp.exp2((scores - top) * scale)
+        total = jnp.sum(probs, axis=1, keepdims=True)
+        o_ref[:, cols] = (dot(probs.astype(BF16), vals) / total).astype(BF16)
+
+
+def local_pair(
+    doc_lengths,
+    ssm_x,
+    ssm_gate,
+    ssm_b,
+    ssm_c,
+    step_size,
+    decay_rate,
+    norm_weight,
+    queries,
+    keys,
+    values,
+):
+    n = lax.axis_size("ctx")
+    index = lax.axis_index("ctx")
+    tp_index = lax.axis_index("tp")
+    parity, pair = index % 2, index // 2
+    first = parity == 0
+    tok = ssm_x.shape[0]
+    rows = 2 * tok
+    group_heads = HEADS // GROUPS
+    groups = step_size.shape[1] // group_heads // 2
+    heads = groups * group_heads
+
+    def half(array, which, axis=1):
+        size = array.shape[axis] // 2
+        return lax.dynamic_slice_in_dim(array, which * size, size, axis)
+
+    def both(array):
+        received = lax.ppermute(half(array, 1 - parity), "ctx", [(j, j ^ 1) for j in range(n)])
+        own = half(array, parity)
+        return jnp.concatenate(stacked(first, own, received), axis=0)
+
+    def skipped(array):
+        return lax.ppermute(array, "ctx", [(j, j + 4) for j in range(n - 4)])
+
+    def crossed(array, far):
+        odd = pair % 2 == 1
+        route = [(j, j + 2) if (j // 2) % 2 == 0 else (j, j - 2) for j in range(n)]
+        return lax.ppermute(jnp.where(odd, far, array), "ctx", route)
+
+    x = both(ssm_x)
+    b = both(ssm_b)
+    step = both(step_size)
+    kv_width = keys.shape[1] // 2
+    own_kv = jnp.concatenate([half(keys, 1 - parity), half(values, 1 - parity)], axis=1)
+    got_kv = lax.ppermute(own_kv, "ctx", [(j, j ^ 1) for j in range(n)])
+    kept_kv = jnp.concatenate([half(keys, parity), half(values, parity)], axis=1)
+    kv = jnp.concatenate(stacked(first, kept_kv, got_kv), axis=0)
+    q = both(queries)
+    c = both(ssm_c)
+    gate = both(ssm_gate)
+
+    starts = doc_starts(doc_lengths)
+    begin = pair * rows
+    positions = begin - 2 * rows + jnp.arange(3 * rows, dtype=jnp.int32)
+    all_docs = doc_index(positions, starts)
+    doc_ids = all_docs[2 * rows :]
+    prev_id = all_docs[2 * rows - 1]
+    dq, dk, dk_all = doc_ids[:, None], doc_ids[None, :], all_docs[None, :]
+
+    log_decay = -(step * half(decay_rate, parity, 0)[None, :])
+    total_decay = jnp.cumsum(log_decay, axis=0)
+    final_sum = total_decay[-1]
+    tail = jnp.exp(final_sum[None] - total_decay) * step
+    tail = tail * (doc_ids == doc_ids[-1]).astype(F32)[:, None]
+    entry = jnp.exp(total_decay) * (doc_ids == prev_id).astype(F32)[:, None]
+    transmit = jnp.exp(final_sum) * (doc_ids[-1] == prev_id).astype(F32)
+
+    def grouped(array):
+        return jnp.transpose(array.reshape(rows, groups, group_heads), (1, 0, 2))
+
+    def grouped_rows(array):
+        return array.T.reshape(groups, group_heads, rows)
+
+    width = x.shape[1] // groups
+    state = b.shape[1] // groups
+    col = pl.BlockSpec((rows, width), lambda g: (0, g))
+    proj = pl.BlockSpec((rows, state), lambda g: (0, g))
+    head_cols = pl.BlockSpec((1, rows, group_heads), lambda g: (g, 0, 0))
+    head_rows = pl.BlockSpec((1, group_heads, rows), lambda g: (g, 0, 0))
+    state_spec = pl.BlockSpec((state, width), lambda g: (0, g))
+    row_spec = pl.BlockSpec((1, width), lambda g: (0, g))
+    dq_spec = pl.BlockSpec((rows, 1), lambda g: (0, 0))
+    dk_spec = pl.BlockSpec((1, rows), lambda g: (0, 0))
+
+    states = []
+    tail_g = grouped(tail)
+    for g in range(groups):
+        states.append(
+            pl.pallas_call(
+                state_kernel,
+                grid=(1,),
+                in_specs=[
+                    pl.BlockSpec((rows, width), lambda _, g=g: (0, g)),
+                    pl.BlockSpec((rows, state), lambda _, g=g: (0, g)),
+                    pl.BlockSpec((1, rows, group_heads), lambda _, g=g: (g, 0, 0)),
+                ],
+                out_specs=pl.BlockSpec((state, width), lambda _: (0, 0)),
+                out_shape=jax.ShapeDtypeStruct((state, width), BF16),
+                scratch_shapes=[pltpu.VMEM((rows, width), BF16)],
+                cost_estimate=pl.CostEstimate(
+                    flops=2 * rows * state * width,
+                    bytes_accessed=2 * (2 * rows * width),
+                    transcendentals=0,
+                ),
+            )(x, b, tail_g)
+        )
+    far_kv = skipped(kv)
+    near_kv = crossed(kv, far_kv)
+    row = transmit[None, :]
+    near_t = lax.ppermute(row, "ctx", [(j, j + 2) for j in range(n - 2)])
+    far_states = [skipped(s) for s in states]
+    near_states = [crossed(s, f) for s, f in zip(states, far_states)]
+
+    total_l = grouped(total_decay)
+    intra = pl.pallas_call(
+        intra_kernel,
+        grid=(groups,),
+        in_specs=[col, proj, proj, head_cols, head_rows, head_rows, dq_spec, dk_spec],
+        out_specs=col,
+        out_shape=jax.ShapeDtypeStruct((rows, groups * width), F32),
+        cost_estimate=pl.CostEstimate(
+            flops=2 * rows * rows * groups * width * 2,
+            bytes_accessed=8 * rows * groups * width,
+            transcendentals=rows * rows * heads,
+        ),
+    )(x, b, c, total_l, grouped_rows(total_decay), grouped_rows(step), dq, dk)
+
+    kv_heads = kv_width // ATT_DIM
+    q_width = q.shape[1] // kv_heads
+
+    def key_spec(k):
+        return pl.BlockSpec((rows, ATT_DIM), lambda h: (0, h + k))
+
+    attended = pl.pallas_call(
+        attention_kernel,
+        grid=(kv_heads,),
+        in_specs=[pl.BlockSpec((rows, q_width), lambda h: (0, h))]
+        + [key_spec(0), key_spec(kv_heads)] * 3
+        + [dq_spec, pl.BlockSpec((1, 3 * rows), lambda h: (0, 0))],
+        out_specs=pl.BlockSpec((rows, q_width), lambda h: (0, h)),
+        out_shape=jax.ShapeDtypeStruct(q.shape, BF16),
+        cost_estimate=pl.CostEstimate(
+            flops=4 * rows * 3 * rows * q.shape[1],
+            bytes_accessed=4 * rows * q.shape[1],
+            transcendentals=rows * 3 * rows * q.shape[1] // ATT_DIM,
+        ),
+    )(q, far_kv, far_kv, near_kv, near_kv, kv, kv, dq, dk_all)
+
+    head_size = width // group_heads
+    wide_t = jnp.repeat(near_t, head_size, axis=1)
+    weight = half(norm_weight, parity, 0)[None, :]
+    entry_g = grouped(entry)
+    tp_size = lax.axis_size("tp")
+    part = rows // 4
+    rank = parity * tp_size + tp_index
+
+    def exchanged(block):
+        pieces = block.reshape(4, part, block.shape[1])
+        got = [(rank, lax.dynamic_index_in_dim(pieces, rank, 0, keepdims=False))]
+        for flip_ctx, flip_tp in ((0, 1), (1, 1), (1, 0)):
+            peer = (parity ^ flip_ctx) * tp_size + (tp_index ^ flip_tp)
+            piece = lax.dynamic_index_in_dim(pieces, peer, 0, keepdims=False)
+            route = [
+                (i * tp_size + j, (i ^ flip_ctx) * tp_size + (j ^ flip_tp))
+                for i in range(n)
+                for j in range(tp_size)
+            ]
+            got.append((peer, lax.ppermute(piece, ("ctx", "tp"), route)))
+        return got
+
+    def placed(blocks):
+        out = jnp.zeros((part, 4 * len(blocks) * blocks[0][0][1].shape[1]), BF16)
+        for k, got in enumerate(blocks):
+            for peer, piece in got:
+                size = piece.shape[1]
+                slot = (peer % tp_size) * 2 + peer // tp_size
+                out = lax.dynamic_update_slice(out, piece, (0, (slot * len(blocks) + k) * size))
+        return out
+
+    attended_blocks = [exchanged(attended)]
+    mixed_blocks = []
+    for g in range(groups):
+        at_g = lambda _, g=g: (0, g)
+        mixed_g = pl.pallas_call(
+            finish_kernel,
+            grid=(1,),
+            in_specs=[
+                pl.BlockSpec((rows, width), at_g),
+                pl.BlockSpec((rows, state), at_g),
+                pl.BlockSpec((state, width), lambda _: (0, 0)),
+                pl.BlockSpec((state, width), lambda _: (0, 0)),
+                pl.BlockSpec((1, width), at_g),
+                pl.BlockSpec((1, rows, group_heads), lambda _, g=g: (g, 0, 0)),
+                pl.BlockSpec((rows, width), at_g),
+                pl.BlockSpec((1, width), at_g),
+            ],
+            out_specs=pl.BlockSpec((rows, width), lambda _: (0, 0)),
+            out_shape=jax.ShapeDtypeStruct((rows, width), BF16),
+            scratch_shapes=[pltpu.VMEM((rows, width), F32)],
+            cost_estimate=pl.CostEstimate(
+                flops=2 * rows * state * width,
+                bytes_accessed=12 * rows * width,
+                transcendentals=rows * width,
+            ),
+        )(intra, c, near_states[g], far_states[g], wide_t, entry_g, gate, weight)
+        mixed_blocks.append(exchanged(mixed_g))
+    return (placed(mixed_blocks), placed(attended_blocks))
+
+
 def solution(mesh):
+    tp = mesh.shape["tp"]
+    paired = tp == 2 and mesh.shape["ctx"] % 4 == 0 and GROUPS // tp % 2 == 0
     return jax.shard_map(
-        local,
+        local_pair if paired else local_any,
         mesh=mesh,
         in_specs=(
             P(),

time: 232 us -> 124 us (0.53)
  the two profiles are of different devices: /device:TPU:19 before, /device:TPU:9 now
where the time goes in v1:
time: 124 us; the launch traced here: 122 us
  starting transfers between devices  27.6 us (22%)
  Pallas kernels  27.2 us (22%)
  local copies, waits for them, and re-layouts  25.5 us (21%)
  waiting for transfers between devices  24.6 us (20%)
  other arithmetic  15.1 us (12%)
  between operations  2.31 us (2%)
    ppermute x3, waiting for transfers between devices, crossed(): return lax.ppermute(jnp.where(odd, far, array), 'ctx', route)  12.3 us
    ppermute x9, starting transfers between devices, exchanged(): got.append((peer, lax.ppermute(piece, ('ctx', 'tp'), route)))  10 us
    ppermute x3, starting transfers between devices, skipped(): return lax.ppermute(array, 'ctx', [(j, j + 4) for j in range(n - 4)])  9.77 us
    dynamic_slice x10, local copies, waits for them, and re-layouts, half(): return lax.dynamic_slice_in_dim(array, which * size, size, axis)  9.57 us
    pallas_call x1, Pallas kernels, local_pair(): pl.pallas_call(attention_kernel, grid=(kv_heads,), in_specs=[pl.BlockSpec...  9.13 us
    ppermute x9, waiting for transfers between devices, exchanged(): got.append((peer, lax.ppermute(piece, ('ctx', 'tp'), route)))  7.22 us
    pallas_call x2, Pallas kernels, local_pair(): pl.pallas_call(finish_kernel, grid=(1,), in_specs=[pl.BlockSpec((rows, wi...  6.89 us
    pallas_call x2, Pallas kernels, local_pair(): pl.pallas_call(state_kernel, grid=(1,), in_specs=[pl.BlockSpec((rows, wid...  5.94 us
  transfers between devices with their start and end apart: 23, of which 7 were waited for; matrix products, arithmetic and copies ran while one was open for 29% of the time, Pallas kernels for 22%

profile of v1, /device:TPU:9, one launch (start us, length us, event | category | flops | bytes accessed | tf_op | source)
XLA Modules:
  0.0 122.3 jit_solution(5100639659183833260)
XLA Ops:
  0.7 1.0 constant_dynamic-slice_fusion.3
  1.7 0.9 constant_dynamic-slice_fusion.2
  2.7 0.7 pad_maximum_fusion.7
  3.3 0.7 collective-permute-start.17
  4.0 1.6 %constant_dynamic-slice_fusion.7 = bf16[128,512]{1,0:T(8,128)(2,1)} fusion(bf16[128,1024]{1,0:T(8,128)(2,1)} %param.15, s32[]{:T(128)S(6)} %select_n.251), kind=kLoop, calls=%fused_computation.64 | loop fusion | bytes 262148 | tf_op jit(solution)/shard_map/dynamic_slice | solution.py:313
  5.6 1.9 %constant_dynamic-slice_fusion.4 = bf16[128,2048]{1,0:T(8,128)(2,1)} fusion(bf16[128,4096]{1,0:T(8,128)(2,1)} %param.19, s32[]{:T(128)S(6)} %select_n.246), kind=kLoop, calls=%fused_computation.55 | loop fusion | bytes 1048580 | tf_op jit(solution)/shard_map/dynamic_slice | solution.py:313
  8.0 0.8 constant_dynamic-slice_fusion.5
  10.3 0.6 fusion.1
  11.0 1.2 compare_convert_fusion
  12.2 0.7 constant_dynamic-slice_fusion.8
  14.6 0.8 copy.30.dq_ref
  15.4 0.7 dynamic_slice.100
  16.2 1.3 %dynamic_slice.103 = f32[2048]{0:T(1024)} dynamic-slice(f32[4096]{0:T(1024)} %param.18, s32[]{:T(128)S(6)} %select_n.245), dynamic_slice_sizes={2048} | dynamic-slice | bytes 16388 | tf_op jit(solution)/shard_map/dynamic_slice | solution.py:313
  17.5 0.7 dynamic-slice_select_fusion.1
  19.3 0.6 exponential_multiply_fusion
  19.9 0.8 copy.31
  20.8 0.8 copy.27
  21.7 0.6 reduce_window_sum.28.lt_ref
  22.4 3.1 %collective-permute-start.6 = (f32[1,32]{0,1:T(8,128)S(1)}, f32[1,32]{0,1:T(8,128)S(1)}, u32[]{:S(2)}, u32[]{:S(2)}) collective-permute-start(f32[1,32]{0,1:T(8,128)S(1)} %get-tuple-element.32), channel_id=1, source_target_pairs={{0,4},{2,6},{4,8},{6,10},{8,12},{10,14},{12,16},{14,18},{16,20},{1... | collective-permute-start | bytes 392 | tf_op jit(solution)/shard_map/ppermute | solution.py:398
  25.5 0.9 copy.32
  26.3 1.4 %collective-permute-done.6 = f32[1,32]{0,1:T(8,128)S(1)} collective-permute-done((f32[1,32]{0,1:T(8,128)S(1)}, f32[1,32]{0,1:T(8,128)S(1)}, u32[]{:S(2)}, u32[]{:S(2)}) %collective-permute-start.6) | collective-permute-done | bytes 160 | tf_op jit(solution)/shard_map/ppermute | solution.py:398
  27.7 1.2 collective-permute-start
  29.1 0.7 broadcast_in_dim.24.t_ref
  29.9 3.2 %collective-permute-start.18 = (bf16[256,512]{1,0:T(8,128)(2,1)S(1)}, bf16[256,512]{1,0:T(8,128)(2,1)S(1)}, u32[]{:S(2)}, u32[]{:S(2)}) collective-permute-start(bf16[256,512]{1,0:T(8,128)(2,1)S(1)} %pad_maximum_fusion.5.k0_ref.v0_ref), channel_id=1, source_target_pairs={{0,8},{2,10},{4,12},{6,14},{8,16},{10,18},{12,20},{14,22},{16,24},... | collective-permute-start | bytes 786440 | tf_op jit(solution)/shard_map/ppermute | solution.py:321
  33.2 1.0 broadcast_select_fusion.14
  34.1 0.7 pad_maximum_fusion.3.b_ref
  34.9 0.7 pad_maximum_fusion.4.c_ref
  35.6 3.6 %collective-permute-done.18.k2_ref.v2_ref = bf16[256,512]{1,0:T(8,128)(2,1)S(1)} collective-permute-done((bf16[256,512]{1,0:T(8,128)(2,1)S(1)}, bf16[256,512]{1,0:T(8,128)(2,1)S(1)}, u32[]{:S(2)}, u32[]{:S(2)}) %collective-permute-start.18) | collective-permute-done | bytes 262176 | tf_op jit(solution)/shard_map/ppermute | solution.py:321
  39.2 0.8 broadcast_select_fusion.8
  40.4 1.3 %broadcast_select_fusion.7 = (bf16[128,2048]{1,0:T(8,128)(2,1)S(1)}, bf16[128,2048]{1,0:T(8,128)(2,1)S(1)}) fusion(bf16[128,2048]{1,0:T(8,128)(2,1)} %collective-permute-done, pred[]{:T(512)S(6)} %eq.40, bf16[128,4096]{1,0:T(8,128)(2,1)S(1)} %copy-done.8, s32[]{:T(128)S(6)} %select_n.245), kind=kLoop, calls=%fused_computation.10 | loop fusion | flops 524288 | bytes 2097157 | tf_op jit(solution)/shard_map/jit(_where)/select_n | solution.py:201
  41.6 1.1 pad_maximum_fusion.x_ref
  42.7 3.0 %shard_map.125 = bf16[256,1024]{1,0:T(8,128)(2,1)} custom-call(bf16[256,2048]{1,0:T(8,128)(2,1)} %pad_maximum_fusion.x_ref, bf16[256,512]{1,0:T(8,128)(2,1)} %pad_maximum_fusion.3.b_ref, f32[2,256,16]{2,1,0:T(8,128)} %bitcast.67), custom_call_target="tpu_custom_call" | custom-call | flops 134217728 | bytes 1048576 | tf_op jit(solution)/shard_map/pallas_call | solution.py:377
  45.7 3.2 %collective-permute-start.11 = (bf16[256,1024]{1,0:T(8,128)(2,1)}, bf16[256,1024]{1,0:T(8,128)(2,1)S(1)}, u32[]{:S(2)}, u32[]{:S(2)}) collective-permute-start(bf16[256,1024]{1,0:T(8,128)(2,1)} %shard_map.125), channel_id=1, source_target_pairs={{0,8},{2,10},{4,12},{6,14},{8,16},{10,18},{12,20},{14,22},{16,24},... | collective-permute-start | bytes 1572872 | tf_op jit(solution)/shard_map/ppermute | solution.py:321
  48.9 2.9 %shard_map.123 = bf16[256,1024]{1,0:T(8,128)(2,1)} custom-call(bf16[256,2048]{1,0:T(8,128)(2,1)} %pad_maximum_fusion.x_ref, bf16[256,512]{1,0:T(8,128)(2,1)} %pad_maximum_fusion.3.b_ref, f32[2,256,16]{2,1,0:T(8,128)} %bitcast.68), custom_call_target="tpu_custom_call" | custom-call | flops 134217728 | bytes 1048576 | tf_op jit(solution)/shard_map/pallas_call | solution.py:377
  51.9 3.4 %collective-permute-start.4 = (bf16[256,1024]{1,0:T(8,128)(2,1)}, bf16[256,1024]{1,0:T(8,128)(2,1)S(1)}, u32[]{:S(2)}, u32[]{:S(2)}) collective-permute-start(bf16[256,1024]{1,0:T(8,128)(2,1)} %shard_map.123), channel_id=1, source_target_pairs={{0,8},{2,10},{4,12},{6,14},{8,16},{10,18},{12,20},{14,22},{16,24},... | collective-permute-start | bytes 1572872 | tf_op jit(solution)/shard_map/ppermute | solution.py:321
  55.3 1.7 %broadcast_select_fusion.3 = (bf16[128,2048]{1,0:T(8,128)(2,1)S(1)}, bf16[128,2048]{1,0:T(8,128)(2,1)S(1)}, bf16[128,2048]{1,0:T(8,128)(2,1)S(1)}, bf16[128,2048]{1,0:T(8,128)(2,1)S(1)}) fusion(bf16[128,2048]{1,0:T(8,128)(2,1)} %collective-permute-done.16, pred[]{:T(512)S(6)} %eq.40, bf16[128,4096]{1,0:T(8,128)(2,1)S(1)} %copy-done.4, s32[]{:T(128)S(6)} %select_n.245, ...), kind=kLoop, calls=%fused_computation.6 | loop fusion | flops 1048576 | bytes 4194309 | tf_op jit(solution)/shard_map/jit(_where)/select_n | solution.py:201
  57.0 1.0 pad_maximum_fusion.2.q_ref
  58.0 1.0 pad_maximum_fusion.1.gate_ref
  59.1 9.1 %shard_map.127 = bf16[256,2048]{1,0:T(8,128)(2,1)} custom-call(bf16[256,2048]{1,0:T(8,128)(2,1)} %pad_maximum_fusion.2.q_ref, bf16[256,512]{1,0:T(8,128)(2,1)} %copy-done.14, bf16[256,512]{1,0:T(8,128)(2,1)} %copy-done.14, bf16[256,512]{1,0:T(8,128)(2,1)} %collective-permute-done.19.k1_ref.v1_ref, bf16[256,512]{1,0:T(8,128)(2,1)} %collective-permute-done.19.k1_ref.v1_ref, ...), custom_call_target="tpu_custom_call" | custom-call | flops 1610612736 | bytes 2097152 | tf_op jit(solution)/shard_map/pallas_call | solution.py:422
  68.2 1.9 %dynamic-slice_bitcast_fusion = (bf16[64,2048]{1,0:T(8,128)(2,1)S(1)}, bf16[64,2048]{1,0:T(8,128)(2,1)}, bf16[64,2048]{1,0:T(8,128)(2,1)S(1)}) fusion(bf16[4,64,2048]{2,1,0:T(8,128)(2,1)} %bitcast.74, s32[]{:T(128)S(6)} %select_n.279, s32[]{:T(128)S(6)} %select_n.275, s32[]{:T(128)S(6)} %select_n.271), kind=kLoop, calls=%fused_computation.15 | loop fusion | bytes 1572876 | tf_op jit(solution)/shard_map/jit(dynamic_index_in_dim)/squeeze | solution.py:450
  70.1 1.2 %collective-permute-start.20 = (bf16[64,2048]{1,0:T(8,128)(2,1)S(1)}, bf16[64,2048]{1,0:T(8,128)(2,1)S(1)}, u32[]{:S(2)}, u32[]{:S(2)}) collective-permute-start(bf16[64,2048]{1,0:T(8,128)(2,1)S(1)} %get-tuple-element.10), channel_id=1, source_target_pairs={{0,1},{1,0},{2,3},{3,2},{4,5},{5,4},{6,7},{7,6},{8,9},{9,8},{10,11... | collective-permute-start | bytes 786440 | tf_op jit(solution)/shard_map/ppermute | solution.py:456
  71.3 5.2 %shard_map.122.y_ref = f32[256,2048]{1,0:T(8,128)} custom-call(bf16[256,2048]{1,0:T(8,128)(2,1)} %pad_maximum_fusion.x_ref, bf16[256,512]{1,0:T(8,128)(2,1)} %pad_maximum_fusion.3.b_ref, bf16[256,512]{1,0:T(8,128)(2,1)} %pad_maximum_fusion.4.c_ref, f32[2,256,16]{2,1,0:T(8,128)} %bitcast.73, f32[2,16,256]{2,1,0:T(8,128)} %reduce_window_sum.28.lt_ref, ...), custom_call_target="tpu_custom_call" | custom-call | flops 536870912 | bytes 4194304 | tf_op jit(solution)/shard_map/pallas_call | solution.py:403
  76.5 2.6 %collective-permute-start.21 = (bf16[64,2048]{1,0:T(8,128)(2,1)}, bf16[64,2048]{1,0:T(8,128)(2,1)S(1)}, u32[]{:S(2)}, u32[]{:S(2)}) collective-permute-start(bf16[64,2048]{1,0:T(8,128)(2,1)} %get-tuple-element.9), channel_id=1, source_target_pairs={{0,3},{1,2},{2,1},{3,0},{4,7},{5,6},{6,5},{7,4},{8,11},{9,10},{10,... | collective-permute-start | bytes 786440 | tf_op jit(solution)/shard_map/ppermute | solution.py:456
  79.2 1.0 bitcast_dynamic-update-slice_fusion
  80.4 1.2 collective-permute-start.5
  81.6 0.9 broadcast_select_fusion
  82.8 2.7 %collective-permute-done.21 = bf16[64,2048]{1,0:T(8,128)(2,1)S(1)} collective-permute-done((bf16[64,2048]{1,0:T(8,128)(2,1)}, bf16[64,2048]{1,0:T(8,128)(2,1)S(1)}, u32[]{:S(2)}, u32[]{:S(2)}) %collective-permute-start.21) | collective-permute-done | bytes 262176 | tf_op jit(solution)/shard_map/ppermute | solution.py:456
  85.7 7.7 %collective-permute-done.5.s1_ref = bf16[256,1024]{1,0:T(8,128)(2,1)S(1)} collective-permute-done((bf16[256,1024]{1,0:T(8,128)(2,1)S(1)}, bf16[256,1024]{1,0:T(8,128)(2,1)S(1)}, u32[]{:S(2)}, u32[]{:S(2)}) %collective-permute-start.5) | collective-permute-done | bytes 524320 | tf_op jit(solution)/shard_map/ppermute | solution.py:326
  93.4 0.8 copy-done.10
  94.2 3.4 %shard_map.124 = bf16[256,1024]{1,0:T(8,128)(2,1)} custom-call(f32[256,2048]{1,0:T(8,128)} %shard_map.122.y_ref, bf16[256,512]{1,0:T(8,128)(2,1)} %pad_maximum_fusion.4.c_ref, bf16[256,1024]{1,0:T(8,128)(2,1)} %copy-done.10, bf16[256,1024]{1,0:T(8,128)(2,1)} %copy-done.1, f32[1,2048]{1,0:T(1,128)} %broadcast_in_dim.24.t_ref, f32[2,256,16]{2,1,0:T(8,128)} %bitcast.65, ...), custom_call_target="tpu_custom_call" | custom-call | flops 134217728 | bytes 3145728 | tf_op jit(solution)/shard_map/pallas_call | solution.py:472
  97.6 1.1 dynamic-slice_bitcast_fusion.6
  98.7 1.3 %collective-permute-start.8 = (bf16[64,1024]{1,0:T(8,128)(2,1)S(1)}, bf16[64,1024]{1,0:T(8,128)(2,1)S(1)}, u32[]{:S(2)}, u32[]{:S(2)}) collective-permute-start(bf16[64,1024]{1,0:T(8,128)(2,1)S(1)} %get-tuple-element.16), channel_id=1, source_target_pairs={{0,1},{1,0},{2,3},{3,2},{4,5},{5,4},{6,7},{7,6},{8,9},{9,8},{10,11... | collective-permute-start | bytes 393224 | tf_op jit(solution)/shard_map/ppermute | solution.py:456
  100.0 4.6 %collective-permute-done.12.s1_ref = bf16[256,1024]{1,0:T(8,128)(2,1)S(1)} collective-permute-done((bf16[256,1024]{1,0:T(8,128)(2,1)}, bf16[256,1024]{1,0:T(8,128)(2,1)S(1)}, u32[]{:S(2)}, u32[]{:S(2)}) %collective-permute-start.12) | collective-permute-done | bytes 524320 | tf_op jit(solution)/shard_map/ppermute | solution.py:326
  104.6 0.8 copy-done.9
  105.4 3.5 %shard_map.126 = bf16[256,1024]{1,0:T(8,128)(2,1)} custom-call(f32[256,2048]{1,0:T(8,128)} %shard_map.122.y_ref, bf16[256,512]{1,0:T(8,128)(2,1)} %pad_maximum_fusion.4.c_ref, bf16[256,1024]{1,0:T(8,128)(2,1)} %copy-done.9, bf16[256,1024]{1,0:T(8,128)(2,1)} %copy-done, f32[1,2048]{1,0:T(1,128)} %broadcast_in_dim.24.t_ref, f32[2,256,16]{2,1,0:T(8,128)} %bitcast.66, ...), custom_call_target="tpu_custom_call" | custom-call | flops 134217728 | bytes 3145728 | tf_op jit(solution)/shard_map/pallas_call | solution.py:472
  108.9 1.1 dynamic-slice_bitcast_fusion.3
  109.9 1.3 %collective-permute-start.13 = (bf16[64,1024]{1,0:T(8,128)(2,1)S(1)}, bf16[64,1024]{1,0:T(8,128)(2,1)S(1)}, u32[]{:S(2)}, u32[]{:S(2)}) collective-permute-start(bf16[64,1024]{1,0:T(8,128)(2,1)S(1)} %get-tuple-element.13), channel_id=1, source_target_pairs={{0,1},{1,0},{2,3},{3,2},{4,5},{5,4},{6,7},{7,6},{8,9},{9,8},{10,11... | collective-permute-start | bytes 393224 | tf_op jit(solution)/shard_map/ppermute | solution.py:456
  111.2 1.8 %collective-permute-start.9 = (bf16[64,1024]{1,0:T(8,128)(2,1)S(1)}, bf16[64,1024]{1,0:T(8,128)(2,1)S(1)}, u32[]{:S(2)}, u32[]{:S(2)}) collective-permute-start(bf16[64,1024]{1,0:T(8,128)(2,1)S(1)} %get-tuple-element.15), channel_id=1, source_target_pairs={{0,3},{1,2},{2,1},{3,0},{4,7},{5,6},{6,5},{7,4},{8,11},{9,10},{10,... | collective-permute-start | bytes 393224 | tf_op jit(solution)/shard_map/ppermute | solution.py:456
  113.1 0.9 bitcast_dynamic-update-slice_fusion.2
  114.1 1.6 %collective-permute-start.14 = (bf16[64,1024]{1,0:T(8,128)(2,1)S(1)}, bf16[64,1024]{1,0:T(8,128)(2,1)S(1)}, u32[]{:S(2)}, u32[]{:S(2)}) collective-permute-start(bf16[64,1024]{1,0:T(8,128)(2,1)S(1)} %get-tuple-element.12), channel_id=1, source_target_pairs={{0,3},{1,2},{2,1},{3,0},{4,7},{5,6},{6,5},{7,4},{8,11},{9,10},{10,... | collective-permute-start | bytes 393224 | tf_op jit(solution)/shard_map/ppermute | solution.py:456
  115.8 3.4 %collective-permute-done.9 = bf16[64,1024]{1,0:T(8,128)(2,1)S(1)} collective-permute-done((bf16[64,1024]{1,0:T(8,128)(2,1)S(1)}, bf16[64,1024]{1,0:T(8,128)(2,1)S(1)}, u32[]{:S(2)}, u32[]{:S(2)}) %collective-permute-start.9) | collective-permute-done | bytes 131104 | tf_op jit(solution)/shard_map/ppermute | solution.py:456
  119.3 0.9 bitcast_dynamic-update-slice_fusion.1
  120.2 1.0 collective-permute-done.14
  121.3 1.0 copy-done.6
  (95 shorter events, 5.4 us)
Async XLA Ops:
  0.6 7.3 %copy-start.5 = (bf16[128,4096]{1,0:T(8,128)(2,1)S(1)}, bf16[128,4096]{1,0:T(8,128)(2,1)}, u32[]{:S(2)}) copy-start(bf16[128,4096]{1,0:T(8,128)(2,1)} %param.13) | copy-start | bytes 3145732
  0.6 8.2 %copy-start.15 = (f32[128,64]{0,1:T(8,128)S(1)}, f32[128,64]{0,1:T(8,128)}, u32[]{:S(2)}) copy-start(f32[128,64]{0,1:T(8,128)} %param.16) | copy-start | bytes 98308
  0.7 9.3 %copy-start.17 = (s32[32]{0:T(128)S(1)}, s32[32]{0:T(128)}, u32[]{:S(2)}) copy-start(s32[32]{0:T(128)} %param.11) | copy-start | bytes 388
  0.7 10.3 %copy-start.8 = (bf16[128,4096]{1,0:T(8,128)(2,1)S(1)}, bf16[128,4096]{1,0:T(8,128)(2,1)}, u32[]{:S(2)}) copy-start(bf16[128,4096]{1,0:T(8,128)(2,1)} %param.12) | copy-start | bytes 3145732
  1.7 10.4 %copy-start.13 = (bf16[128,1024]{1,0:T(8,128)(2,1)S(1)}, bf16[128,1024]{1,0:T(8,128)(2,1)}, u32[]{:S(2)}) copy-start(bf16[128,1024]{1,0:T(8,128)(2,1)} %param.14) | copy-start | bytes 786436
  3.3 26.4 %collective-permute-start.17 = (bf16[128,512]{1,0:T(8,128)(2,1)}, bf16[128,512]{1,0:T(8,128)(2,1)S(1)}, u32[]{:S(2)}, u32[]{:S(2)}) collective-permute-start(bf16[128,512]{1,0:T(8,128)(2,1)} %pad_maximum_fusion.7), channel_id=1, source_target_pairs={{0,2},{2,0},{4,6},{6,4},{8,10},{10,8},{12,14},{14,12},{16,18},{18,... | collective-permute-start | bytes 393224 | tf_op jit(solution)/shard_map/ppermute | solution.py:333
  5.6 24.2 %collective-permute-start.2 = (bf16[128,512]{1,0:T(8,128)(2,1)}, bf16[128,512]{1,0:T(8,128)(2,1)S(1)}, u32[]{:S(2)}, u32[]{:S(2)}) collective-permute-start(bf16[128,512]{1,0:T(8,128)(2,1)} %constant_dynamic-slice_fusion.7), channel_id=1, source_target_pairs={{0,2},{2,0},{4,6},{6,4},{8,10},{10,8},{12,14},{14,12},{16,18},{18,... | collective-permute-start | bytes 393224 | tf_op jit(solution)/shard_map/ppermute | solution.py:316
  7.5 47.8 %collective-permute-start.16 = (bf16[128,2048]{1,0:T(8,128)(2,1)}, bf16[128,2048]{1,0:T(8,128)(2,1)}, u32[]{:S(2)}, u32[]{:S(2)}) collective-permute-start(bf16[128,2048]{1,0:T(8,128)(2,1)} %constant_dynamic-slice_fusion.4), channel_id=1, source_target_pairs={{0,2},{2,0},{4,6},{6,4},{8,10},{10,8},{12,14},{14,12},{16,18},{18,... | collective-permute-start | bytes 1572872 | tf_op jit(solution)/shard_map/ppermute | solution.py:316
  8.8 21.0 %copy-start.11 = (bf16[128,1024]{1,0:T(8,128)(2,1)S(1)}, bf16[128,1024]{1,0:T(8,128)(2,1)}, u32[]{:S(2)}) copy-start(bf16[128,1024]{1,0:T(8,128)(2,1)} %param.15) | copy-start | bytes 786436
  8.8 46.4 %collective-permute-start.7 = (bf16[128,2048]{1,0:T(8,128)(2,1)}, bf16[128,2048]{1,0:T(8,128)(2,1)}, u32[]{:S(2)}, u32[]{:S(2)}) collective-permute-start(bf16[128,2048]{1,0:T(8,128)(2,1)} %constant_dynamic-slice_fusion.5), channel_id=1, source_target_pairs={{0,2},{2,0},{4,6},{6,4},{8,10},{10,8},{12,14},{14,12},{16,18},{18,... | collective-permute-start | bytes 1572872 | tf_op jit(solution)/shard_map/ppermute | solution.py:316
  9.4 8.0 %collective-permute-start.3 = (f32[128,32]{0,1:T(8,128)}, f32[128,32]{0,1:T(8,128)}, u32[]{:S(2)}, u32[]{:S(2)}) collective-permute-start(f32[128,32]{0,1:T(8,128)} %constant_dynamic-slice_fusion.6), channel_id=1, source_target_pairs={{0,2},{2,0},{4,6},{6,4},{8,10},{10,8},{12,14},{14,12},{16,18},{18,... | collective-permute-start | bytes 49160 | tf_op jit(solution)/shard_map/ppermute | solution.py:316
  12.8 21.3 %copy-start.16 = (s32[256]{0:T(256)}, s32[256]{0:T(256)S(1)}, u32[]{:S(2)}) copy-start(s32[256]{0:T(256)S(1)} %slice.22) | copy-start | bytes 3076
  22.4 5.4 %collective-permute-start.6 = (f32[1,32]{0,1:T(8,128)S(1)}, f32[1,32]{0,1:T(8,128)S(1)}, u32[]{:S(2)}, u32[]{:S(2)}) collective-permute-start(f32[1,32]{0,1:T(8,128)S(1)} %get-tuple-element.32), channel_id=1, source_target_pairs={{0,4},{2,6},{4,8},{6,10},{8,12},{10,14},{12,16},{14,18},{16,20},{1... | collective-permute-start | bytes 392 | tf_op jit(solution)/shard_map/ppermute | solution.py:398
  27.7 12.6 %collective-permute-start = (bf16[128,2048]{1,0:T(8,128)(2,1)S(1)}, bf16[128,2048]{1,0:T(8,128)(2,1)}, u32[]{:S(2)}, u32[]{:S(2)}) collective-permute-start(bf16[128,2048]{1,0:T(8,128)(2,1)S(1)} %constant_dynamic-slice_fusion.9), channel_id=1, source_target_pairs={{0,2},{2,0},{4,6},{6,4},{8,10},{10,8},{12,14},{14,12},{16,18},{18,... | collective-permute-start | bytes 1572872 | tf_op jit(solution)/shard_map/ppermute | solution.py:316
  29.8 3.4 %collective-permute-start.1 = (bf16[128,512]{1,0:T(8,128)(2,1)}, bf16[128,512]{1,0:T(8,128)(2,1)S(1)}, u32[]{:S(2)}, u32[]{:S(2)}) collective-permute-start(bf16[128,512]{1,0:T(8,128)(2,1)} %constant_dynamic-slice_fusion.8), channel_id=1, source_target_pairs={{0,2},{2,0},{4,6},{6,4},{8,10},{10,8},{12,14},{14,12},{16,18},{18,... | collective-permute-start | bytes 393224 | tf_op jit(solution)/shard_map/ppermute | solution.py:316
  29.9 11.7 %copy-start.12 = (bf16[256,512]{1,0:T(8,128)(2,1)}, bf16[256,512]{1,0:T(8,128)(2,1)S(1)}, u32[]{:S(2)}) copy-start(bf16[256,512]{1,0:T(8,128)(2,1)S(1)} %pad_maximum_fusion.5.k0_ref.v0_ref) | copy-start | bytes 786436
  29.9 9.3 %collective-permute-start.18 = (bf16[256,512]{1,0:T(8,128)(2,1)S(1)}, bf16[256,512]{1,0:T(8,128)(2,1)S(1)}, u32[]{:S(2)}, u32[]{:S(2)}) collective-permute-start(bf16[256,512]{1,0:T(8,128)(2,1)S(1)} %pad_maximum_fusion.5.k0_ref.v0_ref), channel_id=1, source_target_pairs={{0,8},{2,10},{4,12},{6,14},{8,16},{10,18},{12,20},{14,22},{16,24},... | collective-permute-start | bytes 786440 | tf_op jit(solution)/shard_map/ppermute | solution.py:321
  39.2 1.1 copy-start.14
  40.0 19.0 %collective-permute-start.19 = (bf16[256,512]{1,0:T(8,128)(2,1)}, bf16[256,512]{1,0:T(8,128)(2,1)}, u32[]{:S(2)}, u32[]{:S(2)}) collective-permute-start(bf16[256,512]{1,0:T(8,128)(2,1)} %broadcast_select_fusion.8), channel_id=1, source_target_pairs={{0,4},{2,6},{4,0},{6,2},{8,12},{10,14},{12,8},{14,10},{16,20},{18,... | collective-permute-start | bytes 786440 | tf_op jit(solution)/shard_map/ppermute | solution.py:326
  42.7 12.5 %copy-start.4 = (bf16[128,4096]{1,0:T(8,128)(2,1)S(1)}, bf16[128,4096]{1,0:T(8,128)(2,1)}, u32[]{:S(2)}) copy-start(bf16[128,4096]{1,0:T(8,128)(2,1)} %param.19) | copy-start | bytes 3145732
  45.7 35.8 %collective-permute-start.11 = (bf16[256,1024]{1,0:T(8,128)(2,1)}, bf16[256,1024]{1,0:T(8,128)(2,1)S(1)}, u32[]{:S(2)}, u32[]{:S(2)}) collective-permute-start(bf16[256,1024]{1,0:T(8,128)(2,1)} %shard_map.125), channel_id=1, source_target_pairs={{0,8},{2,10},{4,12},{6,14},{8,16},{10,18},{12,20},{14,22},{16,24},... | collective-permute-start | bytes 1572872 | tf_op jit(solution)/shard_map/ppermute | solution.py:321
  51.9 28.4 %collective-permute-start.4 = (bf16[256,1024]{1,0:T(8,128)(2,1)}, bf16[256,1024]{1,0:T(8,128)(2,1)S(1)}, u32[]{:S(2)}, u32[]{:S(2)}) collective-permute-start(bf16[256,1024]{1,0:T(8,128)(2,1)} %shard_map.123), channel_id=1, source_target_pairs={{0,8},{2,10},{4,12},{6,14},{8,16},{10,18},{12,20},{14,22},{16,24},... | collective-permute-start | bytes 1572872 | tf_op jit(solution)/shard_map/ppermute | solution.py:321
  70.1 10.1 %collective-permute-start.20 = (bf16[64,2048]{1,0:T(8,128)(2,1)S(1)}, bf16[64,2048]{1,0:T(8,128)(2,1)S(1)}, u32[]{:S(2)}, u32[]{:S(2)}) collective-permute-start(bf16[64,2048]{1,0:T(8,128)(2,1)S(1)} %get-tuple-element.10), channel_id=1, source_target_pairs={{0,1},{1,0},{2,3},{3,2},{4,5},{5,4},{6,7},{7,6},{8,9},{9,8},{10,11... | collective-permute-start | bytes 786440 | tf_op jit(solution)/shard_map/ppermute | solution.py:456
  71.3 9.0 %copy-start.3 = (bf16[256,1024]{1,0:T(8,128)(2,1)S(1)}, bf16[256,1024]{1,0:T(8,128)(2,1)}, u32[]{:S(2)}) copy-start(bf16[256,1024]{1,0:T(8,128)(2,1)} %shard_map.123) | copy-start | bytes 1572868
  76.5 5.1 %copy-start.2 = (bf16[256,1024]{1,0:T(8,128)(2,1)S(1)}, bf16[256,1024]{1,0:T(8,128)(2,1)}, u32[]{:S(2)}) copy-start(bf16[256,1024]{1,0:T(8,128)(2,1)} %shard_map.125) | copy-start | bytes 1572868
  76.5 9.1 %collective-permute-start.21 = (bf16[64,2048]{1,0:T(8,128)(2,1)}, bf16[64,2048]{1,0:T(8,128)(2,1)S(1)}, u32[]{:S(2)}, u32[]{:S(2)}) collective-permute-start(bf16[64,2048]{1,0:T(8,128)(2,1)} %get-tuple-element.9), channel_id=1, source_target_pairs={{0,3},{1,2},{2,1},{3,0},{4,7},{5,6},{6,5},{7,4},{8,11},{9,10},{10,... | collective-permute-start | bytes 786440 | tf_op jit(solution)/shard_map/ppermute | solution.py:456
  79.2 6.5 %collective-permute-start.22 = (bf16[64,2048]{1,0:T(8,128)(2,1)S(1)}, bf16[64,2048]{1,0:T(8,128)(2,1)S(1)}, u32[]{:S(2)}, u32[]{:S(2)}) collective-permute-start(bf16[64,2048]{1,0:T(8,128)(2,1)S(1)} %get-tuple-element.8), channel_id=1, source_target_pairs={{0,2},{1,3},{2,0},{3,1},{4,6},{5,7},{6,4},{7,5},{8,10},{9,11},{10,... | collective-permute-start | bytes 786440 | tf_op jit(solution)/shard_map/ppermute | solution.py:456
  80.3 5.4 %copy-start.1 = (bf16[256,1024]{1,0:T(8,128)(2,1)}, bf16[256,1024]{1,0:T(8,128)(2,1)S(1)}, u32[]{:S(2)}) copy-start(bf16[256,1024]{1,0:T(8,128)(2,1)S(1)} %collective-permute-done.4.s2_ref) | copy-start | bytes 1572868
  80.4 13.0 %collective-permute-start.5 = (bf16[256,1024]{1,0:T(8,128)(2,1)S(1)}, bf16[256,1024]{1,0:T(8,128)(2,1)S(1)}, u32[]{:S(2)}, u32[]{:S(2)}) collective-permute-start(bf16[256,1024]{1,0:T(8,128)(2,1)S(1)} %broadcast_select_fusion.1), channel_id=1, source_target_pairs={{0,4},{2,6},{4,0},{6,2},{8,12},{10,14},{12,8},{14,10},{16,20},{18,... | collective-permute-start | bytes 1572872 | tf_op jit(solution)/shard_map/ppermute | solution.py:326
  81.6 16.1 %copy-start = (bf16[256,1024]{1,0:T(8,128)(2,1)}, bf16[256,1024]{1,0:T(8,128)(2,1)S(1)}, u32[]{:S(2)}) copy-start(bf16[256,1024]{1,0:T(8,128)(2,1)S(1)} %collective-permute-done.11.s2_ref) | copy-start | bytes 1572868
  82.5 22.1 %collective-permute-start.12 = (bf16[256,1024]{1,0:T(8,128)(2,1)}, bf16[256,1024]{1,0:T(8,128)(2,1)S(1)}, u32[]{:S(2)}, u32[]{:S(2)}) collective-permute-start(bf16[256,1024]{1,0:T(8,128)(2,1)} %broadcast_select_fusion), channel_id=1, source_target_pairs={{0,4},{2,6},{4,0},{6,2},{8,12},{10,14},{12,8},{14,10},{16,20},{18,... | collective-permute-start | bytes 1572872 | tf_op jit(solution)/shard_map/ppermute | solution.py:326
  85.7 12.0 %copy-start.7 = (bf16[64,8192]{1,0:T(8,128)(2,1)}, bf16[64,8192]{1,0:T(8,128)(2,1)S(1)}, u32[]{:S(2)}) copy-start(bf16[64,8192]{1,0:T(8,128)(2,1)S(1)} %constant_dynamic-update-slice_fusion) | copy-start | bytes 3145732
  93.4 0.8 copy-start.10
  98.7 17.0 %collective-permute-start.8 = (bf16[64,1024]{1,0:T(8,128)(2,1)S(1)}, bf16[64,1024]{1,0:T(8,128)(2,1)S(1)}, u32[]{:S(2)}, u32[]{:S(2)}) collective-permute-start(bf16[64,1024]{1,0:T(8,128)(2,1)S(1)} %get-tuple-element.16), channel_id=1, source_target_pairs={{0,1},{1,0},{2,3},{3,2},{4,5},{5,4},{6,7},{7,6},{8,9},{9,8},{10,11... | collective-permute-start | bytes 393224 | tf_op jit(solution)/shard_map/ppermute | solution.py:456
  104.6 0.8 copy-start.9
  109.9 10.2 %collective-permute-start.13 = (bf16[64,1024]{1,0:T(8,128)(2,1)S(1)}, bf16[64,1024]{1,0:T(8,128)(2,1)S(1)}, u32[]{:S(2)}, u32[]{:S(2)}) collective-permute-start(bf16[64,1024]{1,0:T(8,128)(2,1)S(1)} %get-tuple-element.13), channel_id=1, source_target_pairs={{0,1},{1,0},{2,3},{3,2},{4,5},{5,4},{6,7},{7,6},{8,9},{9,8},{10,11... | collective-permute-start | bytes 393224 | tf_op jit(solution)/shard_map/ppermute | solution.py:456
  111.2 8.0 %collective-permute-start.9 = (bf16[64,1024]{1,0:T(8,128)(2,1)S(1)}, bf16[64,1024]{1,0:T(8,128)(2,1)S(1)}, u32[]{:S(2)}, u32[]{:S(2)}) collective-permute-start(bf16[64,1024]{1,0:T(8,128)(2,1)S(1)} %get-tuple-element.15), channel_id=1, source_target_pairs={{0,3},{1,2},{2,1},{3,0},{4,7},{5,6},{6,5},{7,4},{8,11},{9,10},{10,... | collective-permute-start | bytes 393224 | tf_op jit(solution)/shard_map/ppermute | solution.py:456
  114.0 5.2 %collective-permute-start.10 = (bf16[64,1024]{1,0:T(8,128)(2,1)S(1)}, bf16[64,1024]{1,0:T(8,128)(2,1)S(1)}, u32[]{:S(2)}, u32[]{:S(2)}) collective-permute-start(bf16[64,1024]{1,0:T(8,128)(2,1)S(1)} %get-tuple-element.14), channel_id=1, source_target_pairs={{0,2},{1,3},{2,0},{3,1},{4,6},{5,7},{6,4},{7,5},{8,10},{9,11},{10,... | collective-permute-start | bytes 393224 | tf_op jit(solution)/shard_map/ppermute | solution.py:456
  114.1 7.2 %collective-permute-start.14 = (bf16[64,1024]{1,0:T(8,128)(2,1)S(1)}, bf16[64,1024]{1,0:T(8,128)(2,1)S(1)}, u32[]{:S(2)}, u32[]{:S(2)}) collective-permute-start(bf16[64,1024]{1,0:T(8,128)(2,1)S(1)} %get-tuple-element.12), channel_id=1, source_target_pairs={{0,3},{1,2},{2,1},{3,0},{4,7},{5,6},{6,5},{7,4},{8,11},{9,10},{10,... | collective-permute-start | bytes 393224 | tf_op jit(solution)/shard_map/ppermute | solution.py:456
  115.7 5.6 %collective-permute-start.15 = (bf16[64,1024]{1,0:T(8,128)(2,1)S(1)}, bf16[64,1024]{1,0:T(8,128)(2,1)S(1)}, u32[]{:S(2)}, u32[]{:S(2)}) collective-permute-start(bf16[64,1024]{1,0:T(8,128)(2,1)S(1)} %get-tuple-element.11), channel_id=1, source_target_pairs={{0,2},{1,3},{2,0},{3,1},{4,6},{5,7},{6,4},{7,5},{8,10},{9,11},{10,... | collective-permute-start | bytes 393224 | tf_op jit(solution)/shard_map/ppermute | solution.py:456
  121.3 1.0 copy-start.6

commit v2 on v0

--- a/solution.py
+++ b/solution.py
@@ -1,6 +1,10 @@
+import functools
+
 import jax
 import jax.numpy as jnp
 from jax import lax
+from jax.experimental import pallas as pl
+from jax.experimental.pallas import tpu as pltpu
 from jax.sharding import PartitionSpec as P
 
 HEADS = 128
@@ -112,7 +116,7 @@
     return (new_max, new_sum, running_acc * factor[..., None] + weighted)
 
 
-def local(
+def local_any(
     doc_lengths,
     ssm_x,
     ssm_gate,
@@ -186,9 +190,450 @@
     return (mixed_local, attended_local)
 
 
+LOG2E = 1.4426950408889634
+F32 = jnp.float32
+BF16 = jnp.bfloat16
+MESH_ID = pl.DeviceIdType.MESH
+COLS_LAST = (((1,), (1,)), ((), ()))
+ROWS_FIRST = (((0,), (0,)), ((), ()))
+PIECES = 2
+
+
+def dot(a, b, dims=(((1,), (0,)), ((), ())), precision=None):
+    return lax.dot_general(a, b, dims, precision=precision, preferred_element_type=F32)
+
+
+def spread_heads(columns, head, head_size):
+    lane = lax.broadcasted_iota(jnp.int32, (columns.shape[0], 128), 1)
+    wide = jnp.broadcast_to(columns[:, head : head + 1], lane.shape)
+    for k in range(1, 128 // head_size):
+        wide = jnp.where(lane >= k * head_size, columns[:, head + k : head + k + 1], wide)
+    return wide
+
+
+def pair_kernel(
+    n,
+    lengths,
+    x_in,
+    gate_in,
+    b_in,
+    c_in,
+    step_in,
+    q_in,
+    k_in,
+    v_in,
+    rate_ref,
+    weight_ref,
+    mixed_out,
+    attended_out,
+    x_s,
+    gate_s,
+    b_s,
+    c_s,
+    step_s,
+    q_s,
+    k_s,
+    v_s,
+    s_own,
+    s_far,
+    s_near,
+    t_own,
+    t_far,
+    t_near,
+    y_s,
+    mixed_s,
+    attended_s,
+    bias_s,
+    l_s,
+    lt_s,
+    dtt_s,
+    tail_s,
+    entry_s,
+    send_sem,
+    recv_sem,
+    own_sem,
+):
+    index = lax.axis_index("ctx")
+    tp = lax.axis_index("tp")
+    parity, pair = lax.rem(index, 2), lax.div(index, 2)
+    odd = lax.rem(pair, 2)
+    base = index - parity
+    other = 1 - parity
+    tok = x_in.shape[0]
+    rows = 2 * tok
+    width = x_s.shape[1]
+    group_heads = HEADS // GROUPS
+    heads = step_in.shape[1] // 2
+    groups = heads // group_heads
+    group_width = width // groups
+    state = b_s.shape[1] // groups
+    head_size = width // heads
+    kv_heads = k_s.shape[1] // ATT_DIM
+    q_width = q_s.shape[1] // kv_heads
+    piece = group_width // PIECES
+
+    peers = [
+        (base + other, tp),
+        (index, 1 - tp),
+        (base + other, 1 - tp),
+        (index + 2 - 4 * odd, tp),
+        (lax.rem(index + 4, n), tp),
+        (lax.rem(index + n - 4, n), tp),
+    ]
+    ahead, behind = index + 4 < n, index >= 4
+    barrier = pltpu.get_barrier_semaphore()
+    for peer in peers:
+        pl.semaphore_signal(barrier, inc=1, device_id=peer, device_id_type=MESH_ID)
+    pl.semaphore_wait(barrier, len(peers))
+
+    used = [0, 0]
+
+    def slot():
+        used[0] += 1
+        return used[0] - 1
+
+    def remote(src, dst, peer, k):
+        return pltpu.make_async_remote_copy(
+            src_ref=src,
+            dst_ref=dst,
+            send_sem=send_sem.at[k],
+            recv_sem=recv_sem.at[k],
+            device_id=peer,
+            device_id_type=MESH_ID,
+        )
+
+    def kept(src, dst):
+        used[1] += 1
+        copy = pltpu.make_async_copy(src, dst, own_sem.at[used[1] - 1])
+        copy.start()
+        return copy
+
+    mine = pl.ds(pl.multiple_of(parity * tok, tok), tok)
+    sent = []
+
+    def swap(src, dst, cols=None, skip=0):
+        if cols is None:
+            give, keep, place = src, src, dst.at[pl.ds(pl.multiple_of(parity * tok + skip, tok), tok)]
+        else:
+            begin, size, total = cols
+            give = src.at[:, pl.ds(pl.multiple_of(other * total + begin, 128), size)]
+            keep = src.at[:, pl.ds(pl.multiple_of(parity * total + begin, 128), size)]
+            at = pl.ds(pl.multiple_of(parity * tok + skip, tok), tok)
+            place = dst.at[at, begin : begin + size]
+        copy = remote(give, place, peers[0], slot())
+        copy.start()
+        sent.append(copy)
+        own = kept(keep, place)
+
+        def ready():
+            own.wait()
+            copy.wait_recv()
+
+        return ready
+
+    kv_width = k_s.shape[1]
+    ready_k = swap(k_in, k_s, (0, kv_width, kv_width), 2 * rows)
+    ready_v = swap(v_in, v_s, (0, kv_width, kv_width), 2 * rows)
+    ready_step = swap(step_in, step_s)
+    ready_b = swap(b_in, b_s, (0, b_s.shape[1], b_s.shape[1]))
+    ready_x = [swap(x_in, x_s, (g * group_width, group_width, width)) for g in range(groups)]
+    ready_c = swap(c_in, c_s, (0, c_s.shape[1], c_s.shape[1]))
+    ready_q = swap(q_in, q_s, (0, q_s.shape[1], q_s.shape[1]))
+    ready_gate = swap(gate_in, gate_s, (0, width, width))
+
+    first_pairs = pair < 2
+
+    @pl.when(first_pairs)
+    def _():
+        k_s[:rows, :] = jnp.zeros((rows, kv_width), BF16)
+        v_s[:rows, :] = jnp.zeros((rows, kv_width), BF16)
+        s_far[...] = jnp.zeros_like(s_far)
+        t_far[...] = jnp.zeros_like(t_far)
+
+    def travel(own, far, near):
+        far_slot, near_slot = slot(), slot()
+        to_far = remote(own, far, (index + 4, tp), far_slot)
+        direct = remote(own, near, peers[3], near_slot)
+        relayed = remote(far, near, peers[3], near_slot)
+
+        def start():
+            @pl.when(ahead)
+            def _():
+                to_far.start()
+
+            @pl.when(odd == 0)
+            def _():
+                direct.start()
+
+        def relay():
+            @pl.when(behind)
+            def _():
+                to_far.wait_recv()
+
+            @pl.when(odd == 1)
+            def _():
+                relayed.start()
+
+        def arrive():
+            direct.wait_recv()
+
+        def close():
+            @pl.when(ahead)
+            def _():
+                to_far.wait_send()
+
+            direct.wait_send()
+
+        return start, relay, arrive, close
+
+    own_rows = pl.ds(2 * rows, rows)
+    k_trip = travel(k_s.at[own_rows], k_s.at[pl.ds(0, rows)], k_s.at[pl.ds(rows, rows)])
+    v_trip = travel(v_s.at[own_rows], v_s.at[pl.ds(0, rows)], v_s.at[pl.ds(rows, rows)])
+    t_trip = travel(t_own, t_far, t_near)
+    trips = []
+    for k in range(groups * PIECES):
+        trips.append(travel(s_own.at[k], s_far.at[k], s_near.at[k]))
+
+    ready_k()
+    k_trip[0]()
+    ready_v()
+    v_trip[0]()
+
+    begin = pair * rows
+    row_at = begin - 2 * rows + lax.broadcasted_iota(jnp.int32, (1, 3 * rows), 1)
+    col_at = begin + lax.broadcasted_iota(jnp.int32, (rows, 1), 0)
+    row_doc = jnp.zeros_like(row_at) - 1
+    col_doc = jnp.zeros_like(col_at) - 1
+    begun, prev_id, last_id = jnp.int32(0), jnp.int32(-1), jnp.int32(-1)
+    for j in range(lengths.shape[0]):
+        row_doc += (row_at >= begun).astype(jnp.int32)
+        col_doc += (col_at >= begun).astype(jnp.int32)
+        prev_id += (begin - 1 >= begun).astype(jnp.int32)
+        last_id += (begin + rows - 1 >= begun).astype(jnp.int32)
+        begun = begun + lengths[j]
+    bias_s[...] = jnp.where((row_doc == col_doc) & (row_at <= col_at), 0.0, NEG_LARGE)
+
+    ready_step()
+    low = parity == 0
+    pad = jnp.zeros((rows, 128 - heads), F32)
+    step = jnp.concatenate([jnp.where(low, step_s[:, :heads], step_s[:, heads:]), pad], axis=1)
+    rate = jnp.where(low, rate_ref[:, :heads], rate_ref[:, heads:])
+    rate = jnp.concatenate([rate, pad[:1]], axis=1)
+    at = lax.broadcasted_iota(jnp.int32, (rows, rows), 0)
+    to = lax.broadcasted_iota(jnp.int32, (rows, rows), 1)
+    lower = (to <= at).astype(F32)
+    total_decay = dot(lower, -(step * rate), precision=lax.Precision.HIGHEST)
+    final_sum = total_decay[rows - 1 :, :]
+    l_s[...] = total_decay
+    lt_s[...] = total_decay.T
+    dtt_s[...] = step.T
+    tail_s[...] = jnp.where(col_doc == last_id, jnp.exp(final_sum - total_decay) * step, 0.0)
+    entry_s[...] = jnp.where(col_doc == prev_id, jnp.exp(total_decay), 0.0)
+    passing = (last_id == prev_id).astype(F32)
+    t_own[...] = jnp.broadcast_to(jnp.exp(final_sum) * passing, t_own.shape)
+    t_trip[0]()
+
+    per = 128 // head_size
+    ready_b()
+    for g in range(groups):
+        ready_x[g]()
+        b_t = b_s[:, g * state : (g + 1) * state].T
+        for p in range(PIECES):
+            parts = []
+            for tile in range(piece // 128):
+                lead = g * group_width + p * piece + tile * 128
+                wide = spread_heads(tail_s[...], lead // head_size, head_size)
+                parts.append((x_s[:, lead : lead + 128].astype(F32) * wide).astype(BF16))
+            s_own[g * PIECES + p] = dot(b_t, jnp.concatenate(parts, axis=1)).astype(BF16)
+            trips[g * PIECES + p][0]()
+
+    lane = lax.broadcasted_iota(jnp.int32, (rows, 128), 1)
+    ready_c()
+    for g in range(groups):
+        proj = slice(g * state, (g + 1) * state)
+        inter = dot(c_s[:, proj], b_s[:, proj], COLS_LAST)
+        for tile in range(group_width // 128):
+            lead = g * group_width + tile * 128
+            for k in range(per):
+                h = lead // head_size + k
+                spread = l_s[:, h : h + 1] - lt_s[h : h + 1, :]
+                w = jnp.exp(spread + bias_s[:, 2 * rows :]) * dtt_s[h : h + 1, :]
+                part = dot((w * inter).astype(BF16), x_s[:, lead : lead + 128])
+                whole = part if k == 0 else jnp.where(lane >= k * head_size, part, whole)
+            y_s[:, lead : lead + 128] = whole
+        if g == 0:
+            k_trip[1]()
+            v_trip[1]()
+
+    part_rows = rows // 4
+    leaving = []
+
+    def exchange(src, out, g, size):
+        home = pl.ds(pl.multiple_of((tp * 2 + parity) * groups * size + g * size, 128), size)
+        cols = slice(g * size, (g + 1) * size)
+        for peer, fc, ft in ((peers[1], 0, 1), (peers[2], 1, 1), (peers[0], 1, 0)):
+            rank = (other if fc else parity) * 2 + (1 - tp if ft else tp)
+            at_rows = pl.ds(pl.multiple_of(rank * part_rows, part_rows), part_rows)
+            copy = remote(src.at[at_rows, cols], out.at[:, home], peer, slot())
+            copy.start()
+            leaving.append(copy)
+        at_rows = pl.ds(pl.multiple_of((parity * 2 + tp) * part_rows, part_rows), part_rows)
+        leaving.append(kept(src.at[at_rows, cols], out.at[:, home]))
+
+    scale = LOG2E * ATT_DIM ** (-0.5)
+    ready_q()
+    k_trip[2]()
+    v_trip[2]()
+    for kv_head in range(kv_heads):
+        kv_cols = slice(kv_head * ATT_DIM, (kv_head + 1) * ATT_DIM)
+
+        def one_head(h, carry):
+            cols = pl.ds(pl.multiple_of(kv_head * q_width + h * ATT_DIM, ATT_DIM), ATT_DIM)
+            scores = dot(q_s[:, cols], k_s[:, kv_cols], COLS_LAST) + bias_s[...]
+            top = jnp.max(scores, axis=1, keepdims=True)
+            probs = jnp.exp2((scores - top) * scale)
+            total = jnp.sum(probs, axis=1, keepdims=True)
+            summed = dot(probs.astype(BF16), v_s[:, kv_cols])
+            attended_s[:, cols] = (summed / total).astype(BF16)
+            return carry
+
+        lax.fori_loop(0, q_width // ATT_DIM, one_head, 0)
+        exchange(attended_s, attended_out, kv_head, q_width)
+        if kv_head == 0:
+            t_trip[1]()
+            trips[0][1]()
+        else:
+            trips[1][1]()
+
+    ready_gate()
+    t_trip[2]()
+    for g in range(groups):
+        proj = slice(g * state, (g + 1) * state)
+        square = jnp.zeros((rows, 128), F32)
+        for p in range(PIECES):
+            k = g * PIECES + p
+            if k >= 2:
+                trips[k][1]()
+            trips[k][2]()
+            lead = g * group_width + p * piece
+            decay = jnp.concatenate(
+                [
+                    spread_heads(t_near[...], (lead + tile * 128) // head_size, head_size)[:1]
+                    for tile in range(piece // 128)
+                ],
+                axis=1,
+            )
+            carried = (s_near[k].astype(F32) + decay * s_far[k].astype(F32)).astype(BF16)
+            incoming = dot(c_s[:, proj], carried)
+            for tile in range(piece // 128):
+                cols = slice(lead + tile * 128, lead + tile * 128 + 128)
+                wide = spread_heads(entry_s[...], (lead + tile * 128) // head_size, head_size)
+                z = gate_s[:, cols].astype(F32)
+                total = y_s[:, cols] + incoming[:, tile * 128 : tile * 128 + 128] * wide
+                total = total * (z / (1.0 + jnp.exp(-z)))
+                y_s[:, cols] = total
+                square += total * total
+        mean = jnp.sum(square, axis=1, keepdims=True) * (1.0 / group_width)
+        factor = lax.rsqrt(mean + 1e-05)
+        for tile in range(group_width // 128):
+            lead = g * group_width + tile * 128
+            cols = slice(lead, lead + 128)
+            gain = jnp.where(low, weight_ref[:, cols], weight_ref[:, lead + width : lead + width + 128])
+            mixed_s[:, cols] = (y_s[:, cols] * factor * gain).astype(BF16)
+        exchange(mixed_s, mixed_out, g, group_width)
+
+    for copy in sent:
+        copy.wait_send()
+    for trip in [k_trip, v_trip, t_trip] + trips:
+        trip[3]()
+    for copy in leaving:
+        copy.wait()
+
+
+def local_pair(
+    doc_lengths,
+    ssm_x,
+    ssm_gate,
+    ssm_b,
+    ssm_c,
+    step_size,
+    decay_rate,
+    norm_weight,
+    queries,
+    keys,
+    values,
+):
+    tok, width = ssm_x.shape
+    rows, half = 2 * tok, width // 2
+    groups = step_size.shape[1] * GROUPS // HEADS // 2
+    state = ssm_b.shape[1] // (2 * groups)
+    piece = half // groups // PIECES
+    kv_half = keys.shape[1] // 2
+    q_half = queries.shape[1] // 2
+    pieces = groups * PIECES
+    copies = 9 + groups - 1 + 6 + 2 * pieces + 12
+    any_spec = pl.BlockSpec(memory_space=pl.ANY)
+    vmem_spec = pl.BlockSpec(memory_space=pltpu.VMEM)
+    part = rows // 4
+    scratch = [
+        pltpu.VMEM((rows, half), BF16),
+        pltpu.VMEM((rows, half), BF16),
+        pltpu.VMEM((rows, groups * state), BF16),
+        pltpu.VMEM((rows, groups * state), BF16),
+        pltpu.VMEM((rows, step_size.shape[1]), F32),
+        pltpu.VMEM((rows, q_half), BF16),
+        pltpu.VMEM((3 * rows, kv_half), BF16),
+        pltpu.VMEM((3 * rows, kv_half), BF16),
+        pltpu.VMEM((pieces, state, piece), BF16),
+        pltpu.VMEM((pieces, state, piece), BF16),
+        pltpu.VMEM((pieces, state, piece), BF16),
+        pltpu.VMEM((8, 128), F32),
+        pltpu.VMEM((8, 128), F32),
+        pltpu.VMEM((8, 128), F32),
+        pltpu.VMEM((rows, half), F32),
+        pltpu.VMEM((rows, half), BF16),
+        pltpu.VMEM((rows, q_half), BF16),
+        pltpu.VMEM((rows, 3 * rows), F32),
+        pltpu.VMEM((rows, 128), F32),
+        pltpu.VMEM((128, rows), F32),
+        pltpu.VMEM((128, rows), F32),
+        pltpu.VMEM((rows, 128), F32),
+        pltpu.VMEM((rows, 128), F32),
+        pltpu.SemaphoreType.DMA((copies,)),
+        pltpu.SemaphoreType.DMA((copies,)),
+        pltpu.SemaphoreType.DMA((copies,)),
+    ]
+    mixed, attended = pl.pallas_call(
+        functools.partial(pair_kernel, lax.axis_size("ctx")),
+        out_shape=(
+            jax.ShapeDtypeStruct((part, 4 * half), BF16),
+            jax.ShapeDtypeStruct((part, 4 * q_half), BF16),
+        ),
+        in_specs=[pl.BlockSpec(memory_space=pltpu.SMEM)] + [any_spec] * 8 + [vmem_spec] * 2,
+        out_specs=(any_spec, any_spec),
+        scratch_shapes=scratch,
+        compiler_params=pltpu.CompilerParams(collective_id=0, has_side_effects=True),
+    )(
+        doc_lengths,
+        ssm_x,
+        ssm_gate,
+        ssm_b,
+        ssm_c,
+        step_size,
+        queries,
+        keys,
+        values,
+        decay_rate[None, :],
+        norm_weight[None, :],
+    )
+    return (mixed, attended)
+
+
 def solution(mesh):
+    tp = mesh.shape["tp"]
+    paired = tp == 2 and mesh.shape["ctx"] % 4 == 0 and mesh.shape["ctx"] > 4 and GROUPS // tp % 2 == 0
     return jax.shard_map(
-        local,
+        local_pair if paired else local_any,
         mesh=mesh,
         in_specs=(
             P(),

time: 232 us -> 59 us (0.25)
  the two profiles are of different devices: /device:TPU:19 before, /device:TPU:9 now
where the time goes in v2:
time: 59 us; the launch traced here: 58.7 us
  Pallas kernels  53.2 us (90%)
  local copies, waits for them, and re-layouts  4.81 us (8%)
  between operations  0.65 us (1%)
    pallas_call x1, Pallas kernels, local_pair(): pl.pallas_call(functools.partial(pair_kernel, lax.axis_size('ctx')), out_...  53.2 us
    unnamed x5, local copies, waits for them, and re-layouts  4.81 us

profile of v2, /device:TPU:9, one launch (start us, length us, event | category | flops | bytes accessed | tf_op | source)
XLA Modules:
  0.0 58.7 jit_solution(8248673248074726132)
XLA Ops:
  0.6 1.5 %copy.13.step_in = f32[128,64]{1,0:T(8,128)} copy(f32[128,64]{0,1:T(8,128)} %param.16) | data formatting | bytes 65536 | tf_op args[5]
  2.1 53.2 %shard_map.122 = (bf16[64,8192]{1,0:T(8,128)(2,1)}, bf16[64,8192]{1,0:T(8,128)(2,1)}) custom-call(s32[32]{0:T(128)} %lengths.1, bf16[128,4096]{1,0:T(8,128)(2,1)} %x_in.1, bf16[128,4096]{1,0:T(8,128)(2,1)} %gate_in.1, bf16[128,1024]{1,0:T(8,128)(2,1)} %b_in.1, bf16[128,1024]{1,0:T(8,128)(2,1)} %c_in.1, f32[128,64]{1,0:T(8,128)} %copy.13.step_in, ...), custom_call_target="tpu_custom_call" | custom-call | tf_op jit(solution)/shard_map/pallas_call | solution.py:606
  55.4 0.0 copy-start
  55.4 2.4 %copy.16 = bf16[64,8192]{1,0:T(8,128)(2,1)} copy(bf16[64,8192]{1,0:T(8,128)(2,1)} %get-tuple-element.4) | data formatting | bytes 2097152
  57.7 0.0 copy-done
  57.7 1.0 %copy.17 = bf16[64,8192]{1,0:T(8,128)(2,1)} copy(bf16[64,8192]{1,0:T(8,128)(2,1)S(1)} %copy-done) | data formatting | bytes 2097152
Async XLA Ops:
  55.4 2.4 %copy-start = (bf16[64,8192]{1,0:T(8,128)(2,1)S(1)}, bf16[64,8192]{1,0:T(8,128)(2,1)}, u32[]{:S(2)}) copy-start(bf16[64,8192]{1,0:T(8,128)(2,1)} %get-tuple-element.5) | copy-start | bytes 3145732

commit v3 on v2

--- a/solution.py
+++ b/solution.py
@@ -196,7 +196,9 @@
 MESH_ID = pl.DeviceIdType.MESH
 COLS_LAST = (((1,), (1,)), ((), ()))
 ROWS_FIRST = (((0,), (0,)), ((), ()))
-PIECES = 2
+PIECES = 4
+SHARES = 2
+RELAY_AFTER = (0, 2, 3, None)
 
 
 def dot(a, b, dims=(((1,), (0,)), ((), ())), precision=None):
@@ -263,7 +265,7 @@
     rows = 2 * tok
     width = x_s.shape[1]
     group_heads = HEADS // GROUPS
-    heads = step_in.shape[1] // 2
+    heads = step_in.shape[0] // 2
     groups = heads // group_heads
     group_width = width // groups
     state = b_s.shape[1] // groups
@@ -311,15 +313,12 @@
     mine = pl.ds(pl.multiple_of(parity * tok, tok), tok)
     sent = []
 
-    def swap(src, dst, cols=None, skip=0):
-        if cols is None:
-            give, keep, place = src, src, dst.at[pl.ds(pl.multiple_of(parity * tok + skip, tok), tok)]
-        else:
-            begin, size, total = cols
-            give = src.at[:, pl.ds(pl.multiple_of(other * total + begin, 128), size)]
-            keep = src.at[:, pl.ds(pl.multiple_of(parity * total + begin, 128), size)]
-            at = pl.ds(pl.multiple_of(parity * tok + skip, tok), tok)
-            place = dst.at[at, begin : begin + size]
+    def swap(src, dst, cols, skip=0):
+        begin, size, total = cols
+        give = src.at[:, pl.ds(pl.multiple_of(other * total + begin, 128), size)]
+        keep = src.at[:, pl.ds(pl.multiple_of(parity * total + begin, 128), size)]
+        at = pl.ds(pl.multiple_of(parity * tok + skip, tok), tok)
+        place = dst.at[at, begin : begin + size]
         copy = remote(give, place, peers[0], slot())
         copy.start()
         sent.append(copy)
@@ -334,12 +333,14 @@
     kv_width = k_s.shape[1]
     ready_k = swap(k_in, k_s, (0, kv_width, kv_width), 2 * rows)
     ready_v = swap(v_in, v_s, (0, kv_width, kv_width), 2 * rows)
-    ready_step = swap(step_in, step_s)
+    give_rows = pl.ds(pl.multiple_of(other * heads, 8), heads)
+    keep_rows = pl.ds(pl.multiple_of(parity * heads, 8), heads)
+    copy_step = remote(step_in.at[give_rows], step_s.at[:, mine], peers[0], slot())
+    copy_step.start()
+    sent.append(copy_step)
+    own_step = kept(step_in.at[keep_rows], step_s.at[:, mine])
     ready_b = swap(b_in, b_s, (0, b_s.shape[1], b_s.shape[1]))
     ready_x = [swap(x_in, x_s, (g * group_width, group_width, width)) for g in range(groups)]
-    ready_c = swap(c_in, c_s, (0, c_s.shape[1], c_s.shape[1]))
-    ready_q = swap(q_in, q_s, (0, q_s.shape[1], q_s.shape[1]))
-    ready_gate = swap(gate_in, gate_s, (0, width, width))
 
     first_pairs = pair < 2
 
@@ -366,7 +367,7 @@
                 direct.start()
 
         def relay():
-            @pl.when(behind)
+            @pl.when(behind & (odd == 1))
             def _():
                 to_far.wait_recv()
 
@@ -375,6 +376,10 @@
                 relayed.start()
 
         def arrive():
+            @pl.when(behind & (odd == 0))
+            def _():
+                to_far.wait_recv()
+
             direct.wait_recv()
 
         def close():
@@ -413,12 +418,14 @@
         begun = begun + lengths[j]
     bias_s[...] = jnp.where((row_doc == col_doc) & (row_at <= col_at), 0.0, NEG_LARGE)
 
-    ready_step()
+    own_step.wait()
+    copy_step.wait_recv()
     low = parity == 0
-    pad = jnp.zeros((rows, 128 - heads), F32)
-    step = jnp.concatenate([jnp.where(low, step_s[:, :heads], step_s[:, heads:]), pad], axis=1)
+    pad = jnp.zeros((1, 128 - heads), F32)
+    step_t = jnp.concatenate([step_s[...], jnp.zeros((128 - heads, rows), F32)], axis=0)
+    step = step_t.T
     rate = jnp.where(low, rate_ref[:, :heads], rate_ref[:, heads:])
-    rate = jnp.concatenate([rate, pad[:1]], axis=1)
+    rate = jnp.concatenate([rate, pad], axis=1)
     at = lax.broadcasted_iota(jnp.int32, (rows, rows), 0)
     to = lax.broadcasted_iota(jnp.int32, (rows, rows), 1)
     lower = (to <= at).astype(F32)
@@ -426,7 +433,7 @@
     final_sum = total_decay[rows - 1 :, :]
     l_s[...] = total_decay
     lt_s[...] = total_decay.T
-    dtt_s[...] = step.T
+    dtt_s[...] = step_t
     tail_s[...] = jnp.where(col_doc == last_id, jnp.exp(final_sum - total_decay) * step, 0.0)
     entry_s[...] = jnp.where(col_doc == prev_id, jnp.exp(total_decay), 0.0)
     passing = (last_id == prev_id).astype(F32)
@@ -437,6 +444,10 @@
     ready_b()
     for g in range(groups):
         ready_x[g]()
+        if g == groups - 1:
+            ready_c = swap(c_in, c_s, (0, c_s.shape[1], c_s.shape[1]))
+            ready_q = swap(q_in, q_s, (0, q_s.shape[1], q_s.shape[1]))
+            ready_gate = swap(gate_in, gate_s, (0, width, width))
         b_t = b_s[:, g * state : (g + 1) * state].T
         for p in range(PIECES):
             parts = []
@@ -446,6 +457,7 @@
                 parts.append((x_s[:, lead : lead + 128].astype(F32) * wide).astype(BF16))
             s_own[g * PIECES + p] = dot(b_t, jnp.concatenate(parts, axis=1)).astype(BF16)
             trips[g * PIECES + p][0]()
+        (k_trip, v_trip)[g][1]()
 
     lane = lax.broadcasted_iota(jnp.int32, (rows, 128), 1)
     ready_c()
@@ -461,15 +473,11 @@
                 part = dot((w * inter).astype(BF16), x_s[:, lead : lead + 128])
                 whole = part if k == 0 else jnp.where(lane >= k * head_size, part, whole)
             y_s[:, lead : lead + 128] = whole
-        if g == 0:
-            k_trip[1]()
-            v_trip[1]()
-
     part_rows = rows // 4
     leaving = []
 
-    def exchange(src, out, g, size):
-        home = pl.ds(pl.multiple_of((tp * 2 + parity) * groups * size + g * size, 128), size)
+    def exchange(src, out, g, size, count):
+        home = pl.ds(pl.multiple_of((tp * 2 + parity) * count * size + g * size, 128), size)
         cols = slice(g * size, (g + 1) * size)
         for peer, fc, ft in ((peers[1], 0, 1), (peers[2], 1, 1), (peers[0], 1, 0)):
             rank = (other if fc else parity) * 2 + (1 - tp if ft else tp)
@@ -497,13 +505,16 @@
             attended_s[:, cols] = (summed / total).astype(BF16)
             return carry
 
-        lax.fori_loop(0, q_width // ATT_DIM, one_head, 0)
-        exchange(attended_s, attended_out, kv_head, q_width)
-        if kv_head == 0:
-            t_trip[1]()
-            trips[0][1]()
-        else:
-            trips[1][1]()
+        span = q_width // ATT_DIM // SHARES
+        for share in range(SHARES):
+            lax.fori_loop(share * span, (share + 1) * span, one_head, 0, unroll=2)
+            exchange(attended_s, attended_out, kv_head * SHARES + share, q_width // SHARES, kv_heads * SHARES)
+            done = kv_head * SHARES + share
+            if done == 0:
+                t_trip[1]()
+            for k in range(len(trips)):
+                if RELAY_AFTER[k * 4 // len(trips)] == done:
+                    trips[k][1]()
 
     ready_gate()
     t_trip[2]()
@@ -512,7 +523,7 @@
         square = jnp.zeros((rows, 128), F32)
         for p in range(PIECES):
             k = g * PIECES + p
-            if k >= 2:
+            if RELAY_AFTER[k * 4 // len(trips)] is None:
                 trips[k][1]()
             trips[k][2]()
             lead = g * group_width + p * piece
@@ -540,7 +551,7 @@
             cols = slice(lead, lead + 128)
             gain = jnp.where(low, weight_ref[:, cols], weight_ref[:, lead + width : lead + width + 128])
             mixed_s[:, cols] = (y_s[:, cols] * factor * gain).astype(BF16)
-        exchange(mixed_s, mixed_out, g, group_width)
+        exchange(mixed_s, mixed_out, g, group_width, groups)
 
     for copy in sent:
         copy.wait_send()
@@ -571,7 +582,7 @@
     kv_half = keys.shape[1] // 2
     q_half = queries.shape[1] // 2
     pieces = groups * PIECES
-    copies = 9 + groups - 1 + 6 + 2 * pieces + 12
+    copies = 16 + 2 * pieces + 6 * SHARES + 6
     any_spec = pl.BlockSpec(memory_space=pl.ANY)
     vmem_spec = pl.BlockSpec(memory_space=pltpu.VMEM)
     part = rows // 4
@@ -580,7 +591,7 @@
         pltpu.VMEM((rows, half), BF16),
         pltpu.VMEM((rows, groups * state), BF16),
         pltpu.VMEM((rows, groups * state), BF16),
-        pltpu.VMEM((rows, step_size.shape[1]), F32),
+        pltpu.VMEM((step_size.shape[1] // 2, rows), F32),
         pltpu.VMEM((rows, q_half), BF16),
         pltpu.VMEM((3 * rows, kv_half), BF16),
         pltpu.VMEM((3 * rows, kv_half), BF16),
@@ -619,7 +630,7 @@
         ssm_gate,
         ssm_b,
         ssm_c,
-        step_size,
+        step_size.T,
         queries,
         keys,
         values,

time: 59 us -> 56.3 us (0.954)
  local copies, waits for them, and re-layouts: 4.81 us -> 3.32 us
  Pallas kernels: 53.2 us -> 52 us
    unnamed x5 -> x4, local copies, waits for them, and re-layouts: 4.81 us -> 3.32 us
    pallas_call x1, Pallas kernels: 53.2 us -> 52 us  [local_pair(): pl.pallas_call(functools.partial(pair_kernel, lax.axis_size('ctx')), out_...]
where the time goes in v3:
time: 56.3 us; the launch traced here: 56 us
  Pallas kernels  52 us (92%)
  local copies, waits for them, and re-layouts  3.32 us (6%)
  between operations  0.65 us (1%)
    pallas_call x1, Pallas kernels, local_pair(): pl.pallas_call(functools.partial(pair_kernel, lax.axis_size('ctx')), out_...  52 us
    unnamed x4, local copies, waits for them, and re-layouts  3.32 us

profile of v3, /device:TPU:9, one launch (start us, length us, event | category | flops | bytes accessed | tf_op | source)
XLA Modules:
  0.0 56.0 jit_solution(16639719035167763307)
XLA Ops:
  0.6 52.0 %shard_map.122 = (bf16[64,8192]{1,0:T(8,128)(2,1)}, bf16[64,8192]{1,0:T(8,128)(2,1)}) custom-call(s32[32]{0:T(128)} %lengths.1, bf16[128,4096]{1,0:T(8,128)(2,1)} %x_in.1, bf16[128,4096]{1,0:T(8,128)(2,1)} %gate_in.1, bf16[128,1024]{1,0:T(8,128)(2,1)} %b_in.1, bf16[128,1024]{1,0:T(8,128)(2,1)} %c_in.1, f32[64,128]{1,0:T(8,128)} %bitcast.3, ...), custom_call_target="tpu_custom_call" | custom-call | tf_op jit(solution)/shard_map/pallas_call | solution.py:617
  52.7 0.0 copy-start
  52.7 2.4 %copy.15 = bf16[64,8192]{1,0:T(8,128)(2,1)} copy(bf16[64,8192]{1,0:T(8,128)(2,1)} %get-tuple-element.4) | data formatting | bytes 2097152
  55.0 0.0 copy-done
  55.0 1.0 %copy.16 = bf16[64,8192]{1,0:T(8,128)(2,1)} copy(bf16[64,8192]{1,0:T(8,128)(2,1)S(1)} %copy-done) | data formatting | bytes 2097152
Async XLA Ops:
  52.7 2.4 %copy-start = (bf16[64,8192]{1,0:T(8,128)(2,1)S(1)}, bf16[64,8192]{1,0:T(8,128)(2,1)}, u32[]{:S(2)}) copy-start(bf16[64,8192]{1,0:T(8,128)(2,1)} %get-tuple-element.5) | copy-start | bytes 3145732
